TPU v7x, 32 devices: a whole 2x2x4 slice. The times are simulated.
32 devices in a mesh: dp: 4 (over z), fsdp: 8 (over y, x, core).
Axes of the slice: x: 2, y: 2, z: 4, core: 2. Of those that a mesh axis runs over, the one named last changes fastest.
Arguments:
- hidden: bfloat16 [16384, 2048], P(('dp', 'fsdp')), may hold values from -6 to 6
- out_cotangent: bfloat16 [16384, 2048], P(('dp', 'fsdp')), may hold values from -6 to 6
- norm_gain: bfloat16 [2048], P(('dp', 'fsdp')), may hold values from 0.5 to 1.5
- in_weight: bfloat16 [2048, 8512], P(('dp', 'fsdp')), may hold values from -0.125 to 0.125
- conv_weight: bfloat16 [4352, 4], P('fsdp'), may hold values from -3 to 3
- conv_bias: bfloat16 [4352], P('fsdp'), may hold values from -1.796875 to 1.796875
- step_bias: bfloat16 [64], P('fsdp'), may hold values from -4 to -2
- decay_log: bfloat16 [64], P('fsdp'), may hold values from -7 to 0
- skip_gain: bfloat16 [64], P('fsdp'), may hold values from 0.5 to 1.5
- gate_gain: bfloat16 [4096], P(('dp', 'fsdp')), may hold values from 0.5 to 1.5
- out_weight: bfloat16 [4096, 2048], P(('dp', 'fsdp')), may hold values from -0.09375 to 0.09375
- stretch_len: int32 [64], P(('dp', 'fsdp')), may hold values from 0 to 256, as said below
- stretch_start: int32 [64], P(('dp', 'fsdp')), may hold values from 0 to 1, as said below
Outputs:
- block_out: bfloat16 [16384, 2048], P(('dp', 'fsdp'))
- hidden_grad: float32 [16384, 2048], P(('dp', 'fsdp'))
- norm_gain_grad: float32 [2048], P(('dp', 'fsdp'))
- in_weight_grad: float32 [2048, 8512], P(('dp', 'fsdp'))
- conv_weight_grad: float32 [4352, 4], P('fsdp')
- conv_bias_grad: float32 [4352], P('fsdp')
- step_bias_grad: float32 [64], P('fsdp')
- decay_log_grad: float32 [64], P('fsdp')
- skip_gain_grad: float32 [64], P('fsdp')
- gate_gain_grad: float32 [4096], P(('dp', 'fsdp'))
- out_weight_grad: float32 [4096, 2048], P(('dp', 'fsdp'))
Inputs may be any that keep to these rules, and one draw needn't show every extreme that they name: `stretch_len`: the stretches fall into aligned groups of 16; in each group one sample begins in the group's first stretch or the one after and ends in the group's last 2 stretches, before the group's last stretch; a sample's stretches are full up to one partial stretch and then empty; a sample that takes only the group's first stretch is longer than half of it. `stretch_start`: 1 at the first stretch of every aligned group of 16 stretches, and at the start of the sample that follows a one-stretch sample.
All inputs are finite; a program needn't handle non-finite values.
Results may differ from a plain program's by a relative error of at most 0.011.
Values may be sent and summed in bfloat16 or wider, within the bound.
No kernel may reach another device: no remote copies, remote signals or barrier semaphores. Data moves between devices by JAX's collectives and lax.ppermute only.
A program may use at most 448 MiB of HBM per device.

v0:
```python
import jax
import jax.numpy as jnp
from jax import lax
from jax.sharding import PartitionSpec as P

H = 64
P_SIZE = 64
N = 128
TAPS = 4
STRETCH = 256
DI = 4096
CONV = 4352


PRECISE = lax.Precision.HIGHEST
EPSILON = 1e-05


def shifted(shard, axis, by):
    count = lax.axis_size(axis)
    pairs = [(i, i + by) for i in range(count) if 0 <= i + by < count]
    return lax.ppermute(shard, axis, pairs)


def entering(shard, axis, join, neutral):
    place = lax.axis_index(axis)
    gathered = jax.tree.map(
        lambda a, kind: lax.all_gather(a.astype(kind), axis), shard, (jnp.bfloat16, jnp.bfloat16)
    )
    state = jax.tree.map(lambda a, e: jnp.zeros_like(a) + jnp.asarray(e, a.dtype), shard, neutral)

    def one(step, state):
        return join(
            state,
            jax.tree.map(
                lambda a, own: lax.dynamic_index_in_dim(a, step, 0, False).astype(own.dtype),
                gathered,
                shard,
            ),
        )

    return lax.fori_loop(0, place, one, state)


def carried_in_2(shard, axis, combine, identity):
    count, place = (lax.axis_size(axis), lax.axis_index(axis))
    everything = jax.tree.map(
        lambda part, kind: lax.all_gather(part.astype(kind), axis),
        shard,
        jax.tree.map(lambda a: jnp.bfloat16 if a.dtype == jnp.float32 else a.dtype, shard),
    )
    start = jax.tree.map(
        lambda part, zero: jnp.broadcast_to(jnp.asarray(zero, part.dtype), part.shape),
        shard,
        identity,
    )

    def step(k, before):
        at = count - 1 - k
        reached = at > place
        new = combine(
            before, jax.tree.map(lambda part, own: part[at].astype(own.dtype), everything, shard)
        )
        return jax.tree.map(lambda a, b: jnp.where(reached, a, b), new, before)

    return lax.fori_loop(0, count, step, start)


def as_sent(shard):
    return jax.tree.map(lambda a: a.astype(jnp.bfloat16) if a.dtype == jnp.float32 else a, shard)


def rms_scale(values):
    return lax.rsqrt(jnp.mean(values * values, axis=-1, keepdims=True) + EPSILON)


def gated_norm(mixed, gate_part):
    gated = mixed * jax.nn.silu(gate_part)
    return gated * rms_scale(gated)


def unit_norm(values):
    return values * rms_scale(values)


def convolve(conv_input, edge_rows, weights, conv_bias, row_start, offset):
    row_count = conv_input.shape[0]
    extended = jnp.concatenate([edge_rows, conv_input], axis=0)
    accumulated = conv_bias[None, :] + conv_input * weights[None, :, TAPS - 1]
    for lag_rows in range(1, TAPS):
        keep_mask = 1.0 - row_start * (offset < lag_rows)
        lower = TAPS - 1 - lag_rows
        accumulated = (
            accumulated
            + extended[lower : lower + row_count] * keep_mask[:, None] * weights[None, :, lower]
        )
    return jax.nn.silu(accumulated)


def stretch_terms(values, written, readout, step_size, rates):
    steps = values.shape[0]
    log_decay = jnp.cumsum(step_size * rates[None, :], axis=0)
    scores = jnp.dot(readout, written.T, precision=PRECISE)
    later_mask = (jnp.arange(steps)[:, None] >= jnp.arange(steps)[None, :])[None]
    log_gap = log_decay.T[:, :, None] - log_decay.T[:, None, :]
    decay_map = jnp.where(later_mask, jnp.exp(jnp.where(later_mask, log_gap, 0.0)), 0.0)
    mixing = decay_map * scores[None] * step_size.T[:, None, :]
    inner_out = jnp.einsum("hts,shp->thp", mixing, values, precision=PRECISE)
    tail_weight = jnp.exp(log_decay[-1][None, :] - log_decay) * step_size
    local_state = jnp.einsum(
        "shp,sn->hpn", values * tail_weight[:, :, None], written, precision=PRECISE
    )
    return (inner_out, log_decay, local_state)


def mixer(
    conv_input,
    edge_rows,
    weights,
    conv_bias,
    step_raw,
    step_bias,
    decay_log,
    skip_gain,
    carried_in,
    row_start,
    offset,
    starts,
):
    row_count = conv_input.shape[0]
    activated = convolve(conv_input, edge_rows, weights, conv_bias, row_start, offset)
    values = activated[:, :DI].reshape(row_count, H, P_SIZE)
    written = activated[:, DI : DI + N]
    readout = activated[:, DI + N :]
    step_size = jax.nn.softplus(step_raw + step_bias[None, :])
    rates = -jnp.exp(decay_log)
    nchunk = starts.shape[0]

    def advance(running, pieces):
        end_state, reach_all = running
        stretch_values, stretch_written, stretch_readout, stretch_steps, opening = pieces
        end_state = end_state * (1.0 - opening)
        reach_all = reach_all * (1.0 - opening)
        inner_out, log_decay, local_state = stretch_terms(
            stretch_values, stretch_written, stretch_readout, stretch_steps, rates
        )
        carried = jnp.einsum("tn,hpn->thp", stretch_readout, end_state, precision=PRECISE)
        stretch_out = (
            inner_out
            + jnp.exp(log_decay)[:, :, None] * carried
            + skip_gain[None, :, None] * stretch_values
        )
        weight = reach_all[None, :] * jnp.exp(log_decay)
        end_state = jnp.exp(log_decay[-1])[:, None, None] * end_state + local_state
        reach_all = reach_all * jnp.exp(log_decay[-1])
        return ((end_state, reach_all), (stretch_out, weight))

    initial = (jnp.zeros((H, P_SIZE, N), jnp.float32), jnp.ones((H,), jnp.float32))
    pieces = (
        values.reshape(nchunk, STRETCH, H, P_SIZE),
        written.reshape(nchunk, STRETCH, N),
        readout.reshape(nchunk, STRETCH, N),
        step_size.reshape(nchunk, STRETCH, H),
        starts,
    )
    (end_state, reach_all), (local_out, weight) = lax.scan(jax.checkpoint(advance), initial, pieces)
    local_out = local_out.reshape(row_count, H, P_SIZE)
    weight = weight.reshape(row_count, H)
    carried = jnp.einsum("tn,hpn->thp", readout, carried_in, precision=PRECISE)
    mixed = local_out + weight[:, :, None] * carried
    return (mixed.reshape(row_count, DI), reach_all, end_state, weight, readout)


def link(earlier, later):
    first_decay, first_state = earlier
    next_decay, next_state = later
    return (first_decay * next_decay, next_decay[:, None, None] * first_state + next_state)


def body(
    hidden,
    out_cotangent,
    norm_gain,
    in_weight,
    conv_weight,
    conv_bias,
    step_bias,
    decay_log,
    skip_gain,
    gate_gain,
    out_weight,
    stretch_len,
    stretch_start,
):
    tokens_here = hidden.shape[0]
    gathered = (
        lax.all_gather(norm_gain, "fsdp", axis=0, tiled=True),
        lax.all_gather(in_weight, "fsdp", axis=0, tiled=True),
        lax.all_gather(gate_gain, "fsdp", axis=0, tiled=True),
        lax.all_gather(out_weight, "fsdp", axis=0, tiled=True),
        lax.all_gather(conv_weight, "fsdp", axis=0, tiled=True),
        lax.all_gather(conv_bias, "fsdp", axis=0, tiled=True),
        lax.all_gather(step_bias, "fsdp", axis=0, tiled=True),
        lax.all_gather(decay_log, "fsdp", axis=0, tiled=True),
        lax.all_gather(skip_gain, "fsdp", axis=0, tiled=True),
    )
    norm_group, in_group, gate_group, out_group = (
        gathered[0],
        gathered[1],
        gathered[2],
        gathered[3],
    )
    conv_full, bias_full, step_full, decay_full, skip_full = [
        piece_all.astype(jnp.float32) for piece_all in gathered[4:]
    ]
    offset = jnp.arange(tokens_here) % STRETCH
    starts = stretch_start.astype(jnp.float32)
    row_start = jnp.repeat(starts, STRETCH)
    live_rows = (offset < jnp.repeat(stretch_len, STRETCH)).astype(jnp.float32)
    rows_float = hidden.astype(jnp.float32)
    unit_rows = unit_norm(rows_float)
    gain_piece = lax.all_gather(norm_group, "dp", axis=0, tiled=True)
    weight_piece = lax.all_gather(in_group, "dp", axis=0, tiled=True)
    columns = unit_rows
    inputs = (columns * gain_piece.astype(jnp.float32)[None, :]).astype(jnp.bfloat16)
    summed = jnp.dot(inputs, weight_piece, preferred_element_type=jnp.float32)
    gain_rows = gain_piece
    projected = summed
    norm_full = gain_rows
    gate_part = projected[:, :DI]
    conv_input = projected[:, DI : DI + CONV]
    step_raw = projected[:, DI + CONV :]
    edge_rows = shifted(
        conv_input[tokens_here - (TAPS - 1) :].astype(jnp.bfloat16), "fsdp", 1
    ).astype(jnp.float32)

    def mix_local(
        conv_rows,
        edge_part,
        weights,
        bias_part,
        raw_part,
        step_part,
        decay_part,
        skip_part,
        carried_in,
    ):
        return mixer(
            conv_rows,
            edge_part,
            weights,
            bias_part,
            raw_part,
            step_part,
            decay_part,
            skip_part,
            carried_in,
            row_start,
            offset,
            starts,
        )

    empty_state = jnp.zeros((H, P_SIZE, N), jnp.float32)
    local_out, reach_all, end_state, weight, readout = mix_local(
        conv_input,
        edge_rows,
        conv_full,
        bias_full,
        step_raw,
        step_full,
        decay_full,
        skip_full,
        empty_state,
    )
    _, carried = entering(
        (reach_all, end_state), "fsdp", link, (jnp.ones((H,), jnp.float32), empty_state)
    )
    carried_out = weight[:, :, None] * jnp.einsum(
        "tn,hpn->thp", readout, carried, precision=PRECISE
    )
    mixed = local_out + carried_out.reshape(tokens_here, DI)
    normed = gated_norm(mixed, gate_part)
    gain_piece = lax.all_gather(gate_group, "dp", axis=0, tiled=True)
    weight_piece = lax.all_gather(out_group, "dp", axis=0, tiled=True)
    columns = normed
    inputs = (columns * gain_piece.astype(jnp.float32)[None, :]).astype(jnp.bfloat16)
    summed = jnp.dot(inputs, weight_piece, preferred_element_type=jnp.float32)
    gain_rows = gain_piece
    block_out = (rows_float + live_rows[:, None] * summed).astype(jnp.bfloat16)
    branch_grad = (out_cotangent.astype(jnp.float32) * live_rows[:, None]).astype(jnp.bfloat16)
    grad_g = lax.dot_general(
        branch_grad,
        lax.all_gather(out_group, "dp", axis=0, tiled=True),
        (((1,), (1,)), ((), ())),
        preferred_element_type=jnp.float32,
    )
    gated_low = (normed * gain_rows.astype(jnp.float32)[None, :]).astype(jnp.bfloat16)
    columns = gated_low
    out_weight_grad = lax.psum_scatter(
        lax.dot_general(
            columns, branch_grad, (((0,), (0,)), ((), ())), preferred_element_type=jnp.float32
        ),
        ("dp", "fsdp"),
        scatter_dimension=0,
        tiled=True,
    )
    gate_part_sum = jnp.sum(grad_g * normed, axis=0)
    _, pull_gate = jax.vjp(gated_norm, mixed, gate_part)
    grad_mixed, grad_gate = pull_gate(grad_g * gain_rows.astype(jnp.float32)[None, :])
    grad_heads = grad_mixed.reshape(tokens_here, H, P_SIZE)
    direct = jnp.einsum("thp,tn->hpn", weight[:, :, None] * grad_heads, readout, precision=PRECISE)
    _, later_grad = carried_in_2(
        (reach_all, direct), "fsdp", link, (jnp.ones((H,), jnp.float32), empty_state)
    )
    grad_reach = jnp.sum(later_grad * carried, axis=(1, 2))
    _, pull_mix = jax.vjp(
        mix_local,
        conv_input,
        edge_rows,
        conv_full,
        bias_full,
        step_raw,
        step_full,
        decay_full,
        skip_full,
        carried,
    )
    mix_grads = pull_mix(
        (grad_mixed, grad_reach, later_grad, jnp.zeros_like(weight), jnp.zeros_like(readout))
    )
    (
        grad_conv_input,
        grad_edge,
        grad_conv,
        grad_bias,
        grad_step_raw,
        grad_step,
        grad_decay,
        grad_skip,
        _,
    ) = mix_grads
    from_next = shifted(as_sent(grad_edge), "fsdp", -1).astype(grad_edge.dtype)
    grad_conv_input = grad_conv_input.at[tokens_here - (TAPS - 1) :].add(from_next)
    grad_projected = jnp.concatenate([grad_gate, grad_conv_input, grad_step_raw], axis=1).astype(
        jnp.bfloat16
    )
    grad_inputs = lax.dot_general(
        grad_projected,
        lax.all_gather(in_group, "dp", axis=0, tiled=True),
        (((1,), (1,)), ((), ())),
        preferred_element_type=jnp.float32,
    )
    inputs_low = (unit_rows * norm_full.astype(jnp.float32)[None, :]).astype(jnp.bfloat16)
    columns = inputs_low
    in_weight_grad = lax.psum_scatter(
        lax.dot_general(
            columns, grad_projected, (((0,), (0,)), ((), ())), preferred_element_type=jnp.float32
        ),
        ("dp", "fsdp"),
        scatter_dimension=0,
        tiled=True,
    )
    norm_part_sum = jnp.sum(grad_inputs * unit_rows, axis=0)
    _, pull_norm = jax.vjp(unit_norm, rows_float)
    (grad_rows,) = pull_norm(grad_inputs * norm_full.astype(jnp.float32)[None, :])
    hidden_grad = grad_rows + out_cotangent.astype(jnp.float32)
    reduced = lax.psum(
        (norm_part_sum, gate_part_sum, grad_conv, grad_bias, grad_step, grad_decay, grad_skip),
        ("dp", "fsdp"),
    )
    flat_index = lax.axis_index("dp") * lax.axis_size("fsdp") + lax.axis_index("fsdp")
    inner_index = lax.axis_index("fsdp")
    norm_gain_grad = lax.dynamic_slice_in_dim(
        reduced[0], flat_index * norm_gain.shape[0], norm_gain.shape[0], 0
    )
    gate_gain_grad = lax.dynamic_slice_in_dim(
        reduced[1], flat_index * gate_gain.shape[0], gate_gain.shape[0], 0
    )
    conv_weight_grad = lax.dynamic_slice_in_dim(
        reduced[2], inner_index * conv_weight.shape[0], conv_weight.shape[0], 0
    )
    conv_bias_grad = lax.dynamic_slice_in_dim(
        reduced[3], inner_index * conv_bias.shape[0], conv_bias.shape[0], 0
    )
    step_bias_grad = lax.dynamic_slice_in_dim(
        reduced[4], inner_index * step_bias.shape[0], step_bias.shape[0], 0
    )
    decay_log_grad = lax.dynamic_slice_in_dim(
        reduced[5], inner_index * decay_log.shape[0], decay_log.shape[0], 0
    )
    skip_gain_grad = lax.dynamic_slice_in_dim(
        reduced[6], inner_index * skip_gain.shape[0], skip_gain.shape[0], 0
    )
    return (
        block_out,
        hidden_grad,
        norm_gain_grad,
        in_weight_grad,
        conv_weight_grad,
        conv_bias_grad,
        step_bias_grad,
        decay_log_grad,
        skip_gain_grad,
        gate_gain_grad,
        out_weight_grad,
    )


def solution(mesh):
    placed = (
        P(("dp", "fsdp"), None),
        P(("dp", "fsdp"), None),
        P(("dp", "fsdp")),
        P(("dp", "fsdp"), None),
        P("fsdp", None),
        P("fsdp"),
        P("fsdp"),
        P("fsdp"),
        P("fsdp"),
        P(("dp", "fsdp")),
        P(("dp", "fsdp"), None),
        P(("dp", "fsdp")),
        P(("dp", "fsdp")),
    )
    return jax.shard_map(
        body,
        mesh=mesh,
        in_specs=placed,
        out_specs=(
            P(("dp", "fsdp"), None),
            P(("dp", "fsdp"), None),
            P(("dp", "fsdp")),
            P(("dp", "fsdp"), None),
            P("fsdp", None),
            P("fsdp"),
            P("fsdp"),
            P("fsdp"),
            P("fsdp"),
            P(("dp", "fsdp")),
            P(("dp", "fsdp"), None),
        ),
        check_vma=False,
    )
```

profile of v0, /device:TPU:30, one launch (start us, length us, event | category | flops | bytes accessed | tf_op | source)
XLA Modules:
  0.0 3210.9 jit_solution(10026857266185940891)
XLA Ops:
  8.1 58.0 %all-gather.13.cloned.1.call-done = bf16[512,8512]{1,0:T(8,128)(2,1)} async-done(((bf16[64,8512]{1,0:T(8,128)(2,1)}), bf16[512,8512]{1,0:T(8,128)(2,1)}) %all-gather.13.cloned.1.call-update) | async-done | bytes 8716304 | tf_op jit(solution)/shard_map/all_gather | solution.py:198
  72.9 21.8 all-reduce.20
  95.3 44.1 %all-gather.3 = bf16[4,1,512]{2,1,0:T(2,128)(2,1)S(1)} all-gather(bf16[1,1,512]{2,1,0:T(2,128)(2,1)S(1)} %reshape.515), channel_id=1, replica_groups=mesh['dp'=4,'fsdp'=8] {'dp'}, dimensions={0}, use_global_device_ids=true | all-gather | bytes 5120 | tf_op jit(solution)/shard_map/all_gather | solution.py:222
  147.9 507.3 %all-gather.15.cloned.1.call-done = bf16[2048,8512]{1,0:T(8,128)(2,1)} async-done(((bf16[512,8512]{1,0:T(8,128)(2,1)}), bf16[2048,8512]{1,0:T(8,128)(2,1)}) %all-gather.15.cloned.1.call-update) | async-done | bytes 34865168 | tf_op jit(solution)/shard_map/all_gather | solution.py:223
  655.3 26.2 fusion.162
  697.2 22.8 fusion.125
  753.6 262.6 %while.95 = (s32[]{:T(128)}, f32[64,64,128]{2,1,0:T(8,128)}, f32[64]{0:T(128)S(1)}, f32[2,256,64,64]{1,0,3,2:T(2,128)}, f32[2,256,64]{1,0,2:T(2,128)S(1)}, /*ind...) while((s32[]{:T(128)}, f32[64,64,128]{2,1,0:T(8,128)}, ...), condition=%wide.region_4.5_spmd.clone, body=%wide.region_1.4_spmd.clone.sunk | while | flops 6574719488 | bytes 59323136 | solution.py:166
  759.0 21.0 fusion.269
  800.4 84.3 %dynamic_update_slice.78 = f32[2,256,64,64]{1,0,3,2:T(2,128)} dynamic-update-slice(f32[2,256,64,64]{1,0,3,2:T(2,128)} %get-tuple-element.1813, f32[1,256,64,64]{1,0,3,2:T(1,128)} %copy.391, s32[]{:T(128)S(6)} %copy.432, s32[]{:T(128)} %constant.264.clone.1..sunk.1, s32[]{:T(128)} %constant.264.clone.1..sunk.1, s32[]{:T(128)} %constant.264.clone.1..sunk.1) | dynamic-update-slice | bytes 8388612 | tf_op jit(solution)/shard_map/while/body/jit(dynamic_update_index_in_dim)/dynamic_update_slice | solution.py:166
  889.7 21.0 fusion.269
  931.8 84.3 %dynamic_update_slice.78 = f32[2,256,64,64]{1,0,3,2:T(2,128)} dynamic-update-slice(f32[2,256,64,64]{1,0,3,2:T(2,128)} %get-tuple-element.1813, f32[1,256,64,64]{1,0,3,2:T(1,128)} %copy.391, s32[]{:T(128)S(6)} %copy.432, s32[]{:T(128)} %constant.264.clone.1..sunk.1, s32[]{:T(128)} %constant.264.clone.1..sunk.1, s32[]{:T(128)} %constant.264.clone.1..sunk.1) | dynamic-update-slice | bytes 8388612 | tf_op jit(solution)/shard_map/while/body/jit(dynamic_update_index_in_dim)/dynamic_update_slice | solution.py:166
  1112.8 247.3 %all-gather.19.cloned.1.call-done = bf16[4096,2048]{1,0:T(8,128)(2,1)} async-done(((bf16[1024,2048]{1,0:T(8,128)(2,1)}), bf16[4096,2048]{1,0:T(8,128)(2,1)}) %all-gather.19.cloned.1.call-update) | async-done | bytes 16777232 | tf_op jit(solution)/shard_map/all_gather | solution.py:284
  1360.2 18.3 multiply_reduce_fusion.11
  1404.8 27.0 while.96
  1444.2 14.4 all-gather.23.cloned.1.call-done
  1458.6 14.5 while.97
  1484.8 440.4 %while.98 = (s32[]{:T(128)}, f32[64]{0:T(128)S(1)}, f32[64]{0:T(128)S(1)}, f32[64,64,128]{2,1,0:T(8,128)S(1)}, f32[64]{0:T(128)S(1)}, /*index=5*/f32[2,256,64,64...) while((s32[]{:T(128)}, f32[64]{0:T(128)S(1)}, ...), condition=%wide.region_33.34_spmd.clone, body=%wide.region_17.33_spmd.clone.sunk | while | flops 14903836672 | bytes 147867120 | solution.py:166
  1521.3 28.8 fusion.295
  1574.0 17.7 fusion.300
  1616.5 84.3 %dynamic_update_slice.86 = f32[2,256,64,64]{1,0,3,2:T(2,128)} dynamic-update-slice(f32[2,256,64,64]{1,0,3,2:T(2,128)} %get-tuple-element.1967, f32[1,256,64,64]{1,0,3,2:T(1,128)} %copy.412, s32[]{:T(128)S(6)} %sub.305, s32[]{:T(128)} %constant.264.clone.1..sunk.4, s32[]{:T(128)} %constant.264.clone.1..sunk.4, s32[]{:T(128)} %constant.264.clone.1..sunk.4) | dynamic-update-slice | bytes 8388612 | tf_op jit(solution)/shard_map/transpose(jvp())/while/body/jit(dynamic_update_index_in_dim)/dynamic_update_slice | solution.py:166
  1737.2 28.8 fusion.295
  1790.0 17.7 fusion.300
  1832.7 84.3 %dynamic_update_slice.86 = f32[2,256,64,64]{1,0,3,2:T(2,128)} dynamic-update-slice(f32[2,256,64,64]{1,0,3,2:T(2,128)} %get-tuple-element.1967, f32[1,256,64,64]{1,0,3,2:T(1,128)} %copy.412, s32[]{:T(128)S(6)} %sub.305, s32[]{:T(128)} %constant.264.clone.1..sunk.4, s32[]{:T(128)} %constant.264.clone.1..sunk.4, s32[]{:T(128)} %constant.264.clone.1..sunk.4) | dynamic-update-slice | bytes 8388612 | tf_op jit(solution)/shard_map/transpose(jvp())/while/body/jit(dynamic_update_index_in_dim)/dynamic_update_slice | solution.py:166
  1945.5 25.2 fusion.189
  1971.5 19.0 fusion.157
  1991.2 25.4 fusion.128
  2083.8 33.4 %fusion.145 = f32[2048,8512]{1,0:T(8,128)} fusion(bf16[512,64]{0,1:T(8,128)(2,1)S(1)} %get-tuple-element.1319, bf16[512,4352]{0,1:T(8,128)(2,1)} %convert.22, bf16[512,4096]{0,1:T(8,128)(2,1)} %fusion.128, bf16[512,2048]{1,0:T(8,128)(2,1)S(1)} %copy-done.19, f32[2048]{0:T(1024)S(1)} %bitcast.511, f32[512]{0:T(512)S(1)} %copy-done.68), kind=kOutput, calls=%fused_computation.244 | convolution fusion | flops 17881300992 | bytes 80553984 | tf_op jit(solution)/shard_map/dot_general | solution.py:356
  2117.2 16.2 fusion.140
  2133.5 34.1 %fusion.137 = (f32[2048]{0:T(1024)S(1)}, f32[512]{0:T(512)S(1)}, f32[512,2048]{1,0:T(8,128)}) fusion(bf16[512,2048]{1,0:T(8,128)(2,1)} %param.25, f32[512]{0:T(512)S(1)} %copy-done.68, f32[2048]{0:T(1024)S(1)} %bitcast.512, bf16[2048,8512]{1,0:T(8,128)(2,1)} %all-gather.15.cloned.1.call-done, bf16[512,64]{0,1:T(8,128)(2,1)S(1)} %get-tuple-element.1319, ...), kind=kOutput, calls=%fused_computation.236 | convolution fusion | flops 17884444672 | bytes 49893376 | tf_op jit(solution)/shard_map/dot_general | solution.py:347
  2167.6 47.4 %all-reduce.19 = (f32[2048]{0:T(1024)S(1)}, f32[4352]{0:T(1024)S(1)}, f32[64]{0:T(128)S(1)}, f32[64]{0:T(128)S(1)}, f32[64]{0:T(128)S(1)}, /*index=5*/f32[4096]{0:T(1024)S(1)}) all-reduce(f32[2048]{0:T(1024)S(1)} %get-tuple-element.1187, f32[4352]{0:T(1024)S(1)} %copy-done.44, ...), channel_id=1, replica_groups=mesh['dp'=4,'fsdp'=8] {'dp','fsdp'}, use_global_device_ids=true, to_apply=%region_36.37 | all-reduce | flops 10688 | bytes 85504 | tf_op jit(solution)/shard_map/psum | solution.py:367
  2226.7 231.3 %reduce-scatter.5.cloned.1.call-done = f32[128,2048]{1,0:T(8,128)} async-done(((f32[4096,2048]{1,0:T(8,128)}), f32[128,2048]{1,0:T(8,128)}) %reduce-scatter.5.cloned.1.call-update) | async-done | bytes 1048592 | tf_op jit(solution)/shard_map/reduce_scatter | solution.py:299
  2458.0 745.9 %reduce-scatter.3.cloned.1.call-done = f32[64,8512]{1,0:T(8,128)} async-done(((f32[2048,8512]{1,0:T(8,128)}), f32[64,8512]{1,0:T(8,128)}) %reduce-scatter.3.cloned.1.call-update) | async-done | bytes 2179088 | tf_op jit(solution)/shard_map/reduce_scatter | solution.py:355
  (537 shorter events, 578.5 us)
Async XLA Ops:
  7.2 1012.6 %copy-start = (s32[2]{0:T(128)S(1)}, s32[2]{0:T(128)}, u32[]{:S(2)}) copy-start(s32[2]{0:T(128)} %param.36) | copy-start | bytes 28
  7.3 65.4 %copy-start.72 = (bf16[544]{0:T(1024)(128)(2,1)S(1)}, bf16[544]{0:T(1024)(128)(2,1)}, u32[]{:S(2)}) copy-start(bf16[544]{0:T(1024)(128)(2,1)} %param.30) | copy-start | bytes 3268
  7.3 132.2 %copy-start.69 = (bf16[544,4]{0,1:T(4,128)(2,1)S(1)}, bf16[544,4]{0,1:T(4,128)(2,1)}, u32[]{:S(2)}) copy-start(bf16[544,4]{0,1:T(4,128)(2,1)} %param.29) | copy-start | bytes 13060
  7.3 58.8 %all-gather.13.cloned.1.call-start = ((), (), s32[]{:S(2)}) async-start(), calls=%async_computation.2 | async-start | bytes 9879552 | tf_op jit(solution)/shard_map/all_gather | solution.py:198
  8.0 647.3 %all-gather.15.cloned.1.call-start = ((), (), s32[]{:S(2)}) async-start(), calls=%async_computation.3 | async-start | bytes 43909120 | tf_op jit(solution)/shard_map/all_gather | solution.py:223
  66.1 953.1 %all-gather.17.cloned.1.call-start = ((), (), s32[]{:S(2)}) async-start(), calls=%async_computation.4 | async-start | bytes 4718592 | tf_op jit(solution)/shard_map/all_gather | solution.py:200
  66.8 1007.0 %all-gather.21.cloned.1.call-start = ((), (), s32[]{:S(2)}) async-start(), calls=%async_computation.9 | async-start | bytes 9437184 | tf_op jit(solution)/shard_map/all_gather | solution.py:28
  71.6 610.0 %copy-start.67 = (f32[512]{0:T(512)}, f32[512]{0:T(512)S(1)}, u32[]{:S(2)}) copy-start(f32[512]{0:T(512)S(1)} %fusion.179) | copy-start | bytes 6148
  71.7 625.5 %copy-start.45 = (f32[512]{0:T(512)}, f32[512]{0:T(512)S(1)}, u32[]{:S(2)}) copy-start(f32[512]{0:T(512)S(1)} %get-tuple-element.1357) | copy-start | bytes 6148
  71.7 625.5 %copy-start.47 = (f32[512]{0:T(512)}, f32[512]{0:T(512)S(1)}, u32[]{:S(2)}) copy-start(f32[512]{0:T(512)S(1)} %get-tuple-element.1358) | copy-start | bytes 6148
  71.7 625.5 %copy-start.49 = (f32[512]{0:T(512)}, f32[512]{0:T(512)S(1)}, u32[]{:S(2)}) copy-start(f32[512]{0:T(512)S(1)} %get-tuple-element.1359) | copy-start | bytes 6148
  94.8 586.8 %copy-start.81 = (bf16[64]{0:T(256)(128)(2,1)}, bf16[64]{0:T(256)(128)(2,1)S(1)}, u32[]{:S(2)}) copy-start(bf16[64]{0:T(256)(128)(2,1)S(1)} %get-tuple-element.1307) | copy-start | bytes 388
  94.8 591.4 %copy-start.70 = (f32[64]{0:T(128)}, f32[64]{0:T(128)S(1)}, u32[]{:S(2)}) copy-start(f32[64]{0:T(128)S(1)} %convert_element_type.133) | copy-start | bytes 772
  139.4 542.1 %copy-start.51 = (f32[4,1,512]{2,1,0:T(1,128)}, f32[4,1,512]{2,1,0:T(1,128)S(1)}, u32[]{:S(2)}) copy-start(f32[4,1,512]{2,1,0:T(1,128)S(1)} %convert_element_type.153) | copy-start | bytes 24580
  147.9 549.3 %copy-start.32 = (f32[4352]{0:T(1024)}, f32[4352]{0:T(1024)S(1)}, u32[]{:S(2)}) copy-start(f32[4352]{0:T(1024)S(1)} %get-tuple-element.1189) | copy-start | bytes 52228
  147.9 549.3 %copy-start.34 = (f32[4352]{0:T(1024)}, f32[4352]{0:T(1024)S(1)}, u32[]{:S(2)}) copy-start(f32[4352]{0:T(1024)S(1)} %get-tuple-element.1190) | copy-start | bytes 52228
  147.9 549.3 %copy-start.36 = (f32[4352]{0:T(1024)}, f32[4352]{0:T(1024)S(1)}, u32[]{:S(2)}) copy-start(f32[4352]{0:T(1024)S(1)} %get-tuple-element.1191) | copy-start | bytes 52228
  147.9 549.3 %copy-start.38 = (f32[4352]{0:T(1024)}, f32[4352]{0:T(1024)S(1)}, u32[]{:S(2)}) copy-start(f32[4352]{0:T(1024)S(1)} %get-tuple-element.1192) | copy-start | bytes 52228
  683.9 11.5 collective-permute-start
  1019.1 341.1 %all-gather.19.cloned.1.call-start = ((), (), s32[]{:S(2)}) async-start(), calls=%async_computation.5 | async-start | bytes 20971520 | tf_op jit(solution)/shard_map/all_gather | solution.py:284
  1019.7 438.9 %all-gather.23.cloned.1.call-start = ((), (), s32[]{:S(2)}) async-start(), calls=%async_computation.10 | async-start | bytes 9437184 | tf_op jit(solution)/shard_map/all_gather | solution.py:48
  1038.3 340.3 %copy-start.40 = (f32[4096]{0:T(1024)}, f32[4096]{0:T(1024)S(1)}, u32[]{:S(2)}) copy-start(f32[4096]{0:T(1024)S(1)} %convert_element_type.142) | copy-start | bytes 49156
  1038.3 321.9 %copy-start.73 = (f32[512]{0:T(512)}, f32[512]{0:T(512)S(1)}, u32[]{:S(2)}) copy-start(f32[512]{0:T(512)S(1)} %fusion.178) | copy-start | bytes 6148
  1112.8 265.7 %copy-start.55 = (f32[512]{0:T(512)}, f32[512]{0:T(512)S(1)}, u32[]{:S(2)}) copy-start(f32[512]{0:T(512)S(1)} %fusion.180) | copy-start | bytes 6148
  1403.9 821.4 %all-reduce.23.cloned.1.call-start = ((), (), s32[]{:S(2)}) async-start(), calls=%async_computation.7 | async-start | bytes 139264 | tf_op jit(solution)/shard_map/psum | solution.py:367
  1615.8 85.0 %copy-start.28 = (f32[2,256,128]{2,1,0:T(8,128)}, f32[2,256,128]{2,1,0:T(8,128)S(1)}, u32[]{:S(2)}) copy-start(f32[2,256,128]{2,1,0:T(8,128)S(1)} %fusion.304) | copy-start | bytes 786436 | tf_op jit(solution)/shard_map/transpose(jvp())/while
  1832.0 85.1 %copy-start.28 = (f32[2,256,128]{2,1,0:T(8,128)}, f32[2,256,128]{2,1,0:T(8,128)S(1)}, u32[]{:S(2)}) copy-start(f32[2,256,128]{2,1,0:T(8,128)S(1)} %fusion.304) | copy-start | bytes 786436 | tf_op jit(solution)/shard_map/transpose(jvp())/while
  1971.4 486.5 %reduce-scatter.5.cloned.1.call-start = ((), (), s32[]{:S(2)}) async-start(), calls=%async_computation.8 | async-start | bytes 34603008 | tf_op jit(solution)/shard_map/reduce_scatter | solution.py:299
  1990.6 1213.3 %reduce-scatter.3.cloned.1.call-start = ((), (), s32[]{:S(2)}) async-start(), calls=%async_computation.6 | async-start | bytes 72450048 | tf_op jit(solution)/shard_map/reduce_scatter | solution.py:355
  2042.3 19.6 collective-permute-start.1
  2133.4 85.2 %copy-start.58 = (f32[512]{0:T(512)S(1)}, f32[512]{0:T(512)}, u32[]{:S(2)}) copy-start(f32[512]{0:T(512)} %copy-done.57) | copy-start | bytes 6148
  2133.5 1070.4 %copy-start.1 = (s32[2]{0:T(128)S(1)}, s32[2]{0:T(128)}, u32[]{:S(2)}) copy-start(s32[2]{0:T(128)} %param.36) | copy-start | bytes 28
  (78 other events, 1626.7 us)
Sparse Core Ops, SparseCore 0:
  10.0 56.0 all-gather.12
  67.7 587.5 all-gather.14
  657.2 37.0 all-gather.16
  1019.2 54.5 all-gather.20
  1075.3 284.8 all-gather.18
  1404.1 54.5 all-gather.22
  1971.5 120.1 all-reduce.22
  2094.6 363.3 reduce-scatter.4
  2460.9 742.9 reduce-scatter.2
where the time goes:
time: 3240 us; the launch traced here: 3210 us
  waiting for transfers between devices  1820 us (56%)
  local copies, waits for them, and re-layouts  560 us (17%)
  matrix products  443 us (14%)
  other arithmetic  200 us (6%)
  blocking collectives  150 us (5%)
    reduce_scatter x1, waiting for transfers between devices, body(): lax.psum_scatter(lax.dot_general(columns, grad_projected, (((0,), (0,)),...  746 us
    all_gather x1, waiting for transfers between devices, body(): weight_piece = lax.all_gather(in_group, 'dp', axis=0, tiled=True)  507 us
    dynamic_update_slice x20, local copies, waits for them, and re-layouts, mixer(): lax.scan(jax.checkpoint(advance), initial, pieces)  368 us
    all_gather x1, waiting for transfers between devices, body(): weight_piece = lax.all_gather(out_group, 'dp', axis=0, tiled=True)  247 us
    reduce_scatter x1, waiting for transfers between devices, body(): lax.psum_scatter(lax.dot_general(columns, branch_grad, (((0,), (0,)), (()...  231 us
    dot_general x6, matrix products, stretch_terms(): inner_out = jnp.einsum('hts,shp->thp', mixing, values, precision=PRECISE)  135 us
  transfers between devices with their start and end apart: 11, of which 7 were waited for; matrix products, arithmetic and copies ran while one was open for 20% of the time, Pallas kernels for 0%

commit v1 on v0

v1 whole, which is shorter than its diff:
```python
import functools
import math

import jax
import jax.numpy as jnp
import numpy as np
from jax import lax
from jax.experimental import pallas as pl
from jax.experimental.pallas import tpu as pltpu
from jax.sharding import PartitionSpec as P

H = 64
P_SIZE = 64
N = 128
TAPS = 4
STRETCH = 256
DI = 4096
CONV = 4352
LANES = 128
HALO = 8

EPSILON = 1e-05
BF = jnp.bfloat16
F32 = jnp.float32
VMEM_BYTES = 58 * 1024 * 1024
NEGATIVE = -1e30
PACK = 32
ROWS = 32
HALF = 128


def mm(a, b):
    return lax.dot_general(a, b, (((1,), (0,)), ((), ())), preferred_element_type=F32)


def mm_nt(a, b):
    return lax.dot_general(a, b, (((1,), (1,)), ((), ())), preferred_element_type=F32)


def mm_tn(a, b):
    return lax.dot_general(a, b, (((0,), (0,)), ((), ())), preferred_element_type=F32)


def mm_exact(a, b):
    return lax.dot_general(
        a, b, (((1,), (0,)), ((), ())), precision=lax.Precision.HIGHEST, preferred_element_type=F32
    )


def mm_nt_exact(a, b):
    return lax.dot_general(
        a, b, (((1,), (1,)), ((), ())), precision=lax.Precision.HIGHEST, preferred_element_type=F32
    )


def sigmoid(v):
    return 1.0 / (1.0 + jnp.exp(-v))


def softplus(v):
    return jnp.maximum(v, 0.0) + jnp.log1p(jnp.exp(-jnp.abs(v)))


def half_mask(rows):
    return lax.broadcasted_iota(jnp.int32, (rows, LANES), 1) < P_SIZE


def convolved(ext, taps):
    out = taps[TAPS : TAPS + 1, :]
    for j in range(TAPS):
        low = HALO - (TAPS - 1) + j
        out = out + ext[low : low + STRETCH, :] * taps[j : j + 1, :]
    return out


def three_parts(table, heads_here):
    lane = lax.broadcasted_iota(jnp.int32, table.shape, 1)
    table = jnp.where(lane < heads_here, table, 0.0)
    high = table.astype(BF).astype(F32)
    rest = table - high
    middle = rest.astype(BF).astype(F32)
    low = rest - middle
    packed = high + pltpu.roll(middle, PACK, 1) + pltpu.roll(low, 2 * PACK, 1)
    return packed.astype(BF)


def spreader(heads_here, width):
    source = np.arange(LANES)
    head = np.where(source < 3 * PACK, source % PACK, heads_here)
    return jnp.asarray(head[:, None] == np.arange(heads_here * width)[None, :] // width, BF)


def split_sum(ones, table, heads_here):
    lane = lax.broadcasted_iota(jnp.int32, table.shape, 1)
    got = mm(ones.astype(F32).astype(BF), three_parts(table, heads_here))
    got = got + pltpu.roll(got, LANES - PACK, 1) + pltpu.roll(got, LANES - 2 * PACK, 1)
    return jnp.where(lane < heads_here, got, 0.0)


def lower_ones():
    rows = lax.broadcasted_iota(jnp.int32, (STRETCH, STRETCH), 0)
    cols = lax.broadcasted_iota(jnp.int32, (STRETCH, STRETCH), 1)
    return rows, cols


def forward_kernel(
    starts, hid, gain, w1, taps, heads, skip, to_pairs, to_lanes, u_out, xin_out, dtp_out, mixed_out, sin_out, state, ext,
    scores, mixing, columns, steps,
):
    c = pl.program_id(0)
    fresh = starts[c] > 0
    lanes_v = skip.shape[1]
    lanes_x = taps.shape[1]
    rows_in = hid[...]
    wide = rows_in.astype(F32)
    square = jnp.sum(wide * wide, axis=1, keepdims=True)
    rs = lax.rsqrt(square / rows_in.shape[1] + EPSILON)
    u = (wide * rs * gain[...]).astype(BF)
    u_out[...] = u
    projected = mm(u, w1[...])
    conv_input = projected[:, :lanes_x]
    dtp = projected[:, lanes_x:] + heads[0:1, :]
    xin_out[...] = conv_input
    dtp_out[...] = dtp
    halo = ext[pl.ds(STRETCH, HALO), :]
    ext[pl.ds(0, HALO), :] = jnp.where(fresh, 0.0, halo)
    ext[pl.ds(HALO, STRETCH), :] = conv_input
    pre = convolved(ext, taps)
    act = pre * sigmoid(pre)
    values = act[:, :lanes_v]
    written = act[:, lanes_v : lanes_v + N].astype(BF)
    readout = act[:, lanes_v + N :].astype(BF)
    step = softplus(dtp)
    rows, cols = lower_ones()
    causal = rows >= cols
    decay = split_sum(causal, step * heads[1:2, :], lanes_v // P_SIZE)
    decay_t = decay.T
    before = jnp.where(fresh, 0.0, state[...])
    sin_out[0] = before
    scores[...] = mm_nt(readout, written)
    columns[...] = mm(three_parts(decay, lanes_v // P_SIZE), to_lanes[...])
    steps[...] = mm(three_parts(step, lanes_v // P_SIZE), to_pairs[...])
    carried = mm(readout, before.astype(BF))
    written_t = act[:, lanes_v : lanes_v + N].T.astype(BF)
    left = half_mask(STRETCH)
    for pair in range(lanes_v // LANES):
        lo = pair * LANES
        v = values[:, lo : lo + LANES]
        step_pair = steps[:, lo : lo + LANES]
        decay_pair = jnp.where(
            left, columns[:, 2 * lo : 2 * lo + LANES], columns[:, 2 * lo + LANES : 2 * (lo + LANES)]
        )
        last_pair = decay_pair[STRETCH - 1 :, :]
        sv_wide = v * step_pair
        sv = sv_wide.astype(BF)
        out = jnp.exp(decay_pair) * carried[:, lo : lo + LANES] + skip[:, lo : lo + LANES] * v
        top, bottom = out[:HALF], out[HALF:]
        for j in range(2):
            h = 2 * pair + j
            for r in range(0, STRETCH, ROWS):
                column = columns[r : r + ROWS, h * HALF : (h + 1) * HALF]
                for t in range(0, HALF if r < HALF else STRETCH, HALF):
                    gap = column - decay_t[h : h + 1, t : t + HALF]
                    if t + HALF > r:
                        gap = jnp.where(block_mask(r, t), gap, NEGATIVE)
                    block = scores[r : r + ROWS, t : t + HALF] * jnp.exp(gap)
                    mixing[j, r : r + ROWS, t : t + HALF] = block.astype(BF)
            mine = left if j == 0 else jnp.logical_not(left)
            sv_mine = jnp.where(mine, sv, jnp.zeros_like(sv))
            top = top + mm(mixing[j, :HALF, :HALF], sv_mine[:HALF])
            bottom = bottom + mm(mixing[j, HALF:, :], sv_mine)
        mixed_out[:HALF, lo : lo + LANES] = top
        mixed_out[HALF:, lo : lo + LANES] = bottom
        tv = (sv_wide * jnp.exp(last_pair - decay_pair)).astype(BF)
        state[:, lo : lo + LANES] = jnp.exp(last_pair) * before[:, lo : lo + LANES] + mm(
            written_t, tv
        )


def block_mask(r, t):
    rows = lax.broadcasted_iota(jnp.int32, (ROWS, HALF), 0) + r
    cols = lax.broadcasted_iota(jnp.int32, (ROWS, HALF), 1) + t
    return rows >= cols


def block_mask_t(r, t):
    rows = lax.broadcasted_iota(jnp.int32, (ROWS, HALF), 0) + r
    cols = lax.broadcasted_iota(jnp.int32, (ROWS, HALF), 1) + t
    return rows <= cols


def column_rows(column):
    wide = jnp.broadcast_to(column, (STRETCH, LANES))
    return wide.T[0:8, :]


def gate_kernel(u, wg, ow, mixed, gain, branch_out, gate_out, squares_out):
    gate = mm(u[...], wg[...])
    gate_out[...] = gate
    gated = mixed[...] * gate * sigmoid(gate)
    branch_out[...] = mm((gated * gain[...]).astype(BF), ow[...]).astype(BF)
    squares_out[...] = column_rows(jnp.sum(gated * gated, axis=1, keepdims=True))


def pull_kernel(lengths, cot, ow, gate, mixed, gain, gg_out, along_out):
    c = pl.program_id(0)
    alive = lax.broadcasted_iota(jnp.int32, (STRETCH, 1), 0) < lengths[c]
    cotangent = cot[...]
    cotangent = jnp.where(alive, cotangent, jnp.zeros_like(cotangent))
    gg = mm_nt(cotangent, ow[...])
    gg_out[...] = gg
    gated = mixed[...] * gate[...] * sigmoid(gate[...])
    along_out[...] = column_rows(jnp.sum(gg * gain[...] * gated, axis=1, keepdims=True))


def gate_back_kernel(
    outer,
    lengths,
    hid,
    cot,
    gate,
    gg,
    mixed,
    stats,
    gain,
    dmix_out,
    dgate_out,
    ggg_out,
    *rest,
):
    c = pl.program_id(0)
    outs, (owg, iwg) = rest[:-2], rest[-2:]
    count = pl.num_programs(0)
    iwg_outs = outs[:outer]
    owg_outs = outs[outer:]
    r = stats[:, 0:1]
    m = stats[:, 1:2]
    v = gate[...]
    s = sigmoid(v)
    silu = v * s
    mix = mixed[...]
    normed = mix * silu * r
    back = gg[...]
    dgated = r * (back * gain[...] - normed * m)
    dmix_out[...] = dgated * silu
    dgate = dgated * mix * (s * (1.0 + v * (1.0 - s)))
    dgate_low = dgate.astype(BF)
    dgate_out[...] = dgate_low
    alive = lax.broadcasted_iota(jnp.int32, (STRETCH, 1), 0) < lengths[c]
    cotangent = cot[...]
    cotangent = jnp.where(alive, cotangent, jnp.zeros_like(cotangent))
    owg_part = mm_tn((normed * gain[...]).astype(BF), cotangent)
    iwg_part = mm_tn(hid[...], dgate_low)
    ggg_part = jnp.sum(back * normed, axis=0, keepdims=True)

    @pl.when(c == 0)
    def _():
        owg[...] = owg_part
        iwg[...] = iwg_part
        ggg_out[...] = ggg_part

    @pl.when(c > 0)
    def _():
        owg[...] += owg_part
        iwg[...] += iwg_part
        ggg_out[...] += ggg_part

    @pl.when(c == pl.num_programs(0) - 1)
    def _():
        for whole, parts in ((owg, owg_outs), (iwg, iwg_outs)):
            rows = whole.shape[0] // len(parts)
            for k, out in enumerate(parts):
                at = lax.rem(lengths[count] + k, len(parts)) * rows
                out[...] = whole[pl.ds(pl.multiple_of(at, 16), rows), :].astype(BF)


def backward_kernel(
    starts,
    xin,
    xprev,
    dtp_in,
    dmix,
    dgate,
    sin,
    w1,
    wg,
    taps,
    heads,
    skip,
    to_pairs,
    to_lanes,
    f_out,
    gpv_out,
    gps_out,
    conv_out,
    head_out,
    skip_out,
    dstate,
    ext,
    gext,
    gbuf,
    scores,
    dscores,
    dmixing,
    mixing,
    row_sums,
    col_sums,
    columns,
    steps,
):
    step_id = pl.program_id(0)
    count = pl.num_programs(0)
    c = count - 1 - step_id
    fresh = starts[c] > 0
    lanes_v = skip.shape[1]
    lanes_x = taps.shape[1]
    first = step_id == 0
    next_fresh = jnp.logical_or(first, starts[jnp.minimum(c + 1, count - 1)] > 0)

    ext[pl.ds(0, HALO), :] = jnp.where(fresh, 0.0, xprev[...])
    ext[pl.ds(HALO, STRETCH), :] = xin[...]
    pre = convolved(ext, taps)
    sig = sigmoid(pre)
    act = pre * sig
    values = act[:, :lanes_v]
    written_f = act[:, lanes_v : lanes_v + N]
    readout_f = act[:, lanes_v + N :]
    written = written_f.astype(BF)
    readout = readout_f.astype(BF)
    dtp = dtp_in[...]
    step = softplus(dtp)
    rate = heads[1:2, :]
    rows, cols = lower_ones()
    causal = rows >= cols
    anti = rows <= cols
    decay = split_sum(causal, step * rate, lanes_v // P_SIZE)
    decay_t = decay.T
    last = decay[STRETCH - 1 : STRETCH, :]
    grow_last = jnp.exp(last)
    before = sin[0]
    before_low = before.astype(BF)
    after = jnp.where(next_fresh, 0.0, dstate[...])
    after_low = after.astype(BF)
    scores[...] = mm_nt(written, readout)
    columns[...] = mm(three_parts(decay, lanes_v // P_SIZE), to_lanes[...])
    steps[...] = mm(three_parts(step, lanes_v // P_SIZE), to_pairs[...])
    carried = mm(readout, before_low)
    spread = mm(written, after_low)
    readout_t = readout_f.T.astype(BF)
    left = half_mask(STRETCH)
    left_row = half_mask(1)
    lane = lax.broadcasted_iota(jnp.int32, (STRETCH, LANES), 1)
    lane_row = lax.broadcasted_iota(jnp.int32, (1, LANES), 1)
    row_sums[...] = jnp.zeros_like(row_sums)
    lane_rows = lax.broadcasted_iota(jnp.int32, (ROWS, LANES), 1)
    within = jnp.zeros((STRETCH, LANES), F32)
    inner = jnp.zeros((STRETCH, LANES), F32)
    direct = jnp.zeros((STRETCH, LANES), F32)
    through = jnp.zeros((1, LANES), F32)
    dwritten = jnp.zeros((STRETCH, N), F32)
    dreadout = jnp.zeros((STRETCH, N), F32)
    for pair in range(lanes_v // LANES):
        lo = pair * LANES
        v = values[:, lo : lo + LANES]
        dy = dmix[:, lo : lo + LANES]
        step_pair = steps[:, lo : lo + LANES]
        decay_pair = jnp.where(
            left, columns[:, 2 * lo : 2 * lo + LANES], columns[:, 2 * lo + LANES : 2 * (lo + LANES)]
        )
        last_pair = decay_pair[STRETCH - 1 :, :]
        fall_pair = jnp.exp(last_pair - decay_pair)
        sv = v * step_pair
        sv_low = sv.astype(BF)
        dy_low = dy.astype(BF)
        q = fall_pair * spread[:, lo : lo + LANES]
        flow = sv * q
        grown = dy * jnp.exp(decay_pair)
        enter = grown * carried[:, lo : lo + LANES]
        top, bottom = q[:HALF], q[HALF:]
        for j in range(2):
            h = 2 * pair + j
            mine = left if j == 0 else jnp.logical_not(left)
            low_mine = jnp.where(mine, dy_low, jnp.zeros_like(dy_low))
            dmixing[j, :HALF, :] = mm_nt(sv_low[:HALF], low_mine)
            dmixing[j, HALF:, HALF:] = mm_nt(sv_low[HALF:], low_mine[HALF:])
            sums = [jnp.zeros((8, HALF), F32), jnp.zeros((8, HALF), F32)]
            for r in range(0, STRETCH, ROWS):
                column = columns[r : r + ROWS, h * HALF : (h + 1) * HALF]
                across = jnp.zeros((ROWS, HALF), F32)
                for t in range(0 if r < HALF else HALF, STRETCH, HALF):
                    gap = decay_t[h : h + 1, t : t + HALF] - column
                    if t < r + ROWS:
                        gap = jnp.where(block_mask_t(r, t), gap, NEGATIVE)
                    kernel = jnp.exp(gap)
                    block = scores[r : r + ROWS, t : t + HALF] * kernel
                    back = dmixing[j, r : r + ROWS, t : t + HALF]
                    mixing[j, r : r + ROWS, t : t + HALF] = block.astype(BF)
                    turned = kernel * back
                    if h:
                        turned = turned + dscores[r : r + ROWS, t : t + HALF]
                    dscores[r : r + ROWS, t : t + HALF] = turned
                    edges = block * back
                    across = across + edges
                    for k in range(0, ROWS, 8):
                        sums[t // HALF] = sums[t // HALF] + edges[k : k + 8]
                total = jnp.sum(across, axis=1, keepdims=True)
                old = col_sums[r : r + ROWS, :] if h else jnp.zeros((ROWS, LANES), F32)
                col_sums[r : r + ROWS, :] = jnp.where(lane_rows == h, total, old)
            row_sums[h : h + 1, :HALF] = jnp.sum(sums[0], axis=0, keepdims=True)
            row_sums[h : h + 1, HALF:] = jnp.sum(sums[1], axis=0, keepdims=True)
            top = top + mm(mixing[j, :HALF, :], low_mine)
            bottom = bottom + mm(mixing[j, HALF:, HALF:], low_mine[HALF:])
            zero = jnp.zeros_like(flow)
            within = jnp.where(
                lane == h, jnp.sum(jnp.where(mine, flow, zero), axis=1, keepdims=True), within
            )
            inner = jnp.where(
                lane == h, jnp.sum(jnp.where(mine, enter, zero), axis=1, keepdims=True), inner
            )
        q = jnp.concatenate([top, bottom], axis=0)
        vq = v * q
        cross = jnp.sum(
            before[:, lo : lo + LANES] * after[:, lo : lo + LANES], axis=0, keepdims=True
        )
        for j in range(2):
            h = 2 * pair + j
            mine = left if j == 0 else jnp.logical_not(left)
            mine_row = left_row if j == 0 else jnp.logical_not(left_row)
            direct = jnp.where(
                lane == h, jnp.sum(jnp.where(mine, vq, 0.0), axis=1, keepdims=True), direct
            )
            through = jnp.where(
                lane_row == h,
                jnp.sum(jnp.where(mine_row, cross, 0.0), axis=1, keepdims=True),
                through,
            )
        gbuf[:, lo : lo + LANES] = step_pair * q + skip[:, lo : lo + LANES] * dy
        skip_part = jnp.sum(dy * v, axis=0, keepdims=True)
        skip_out[0:1, lo : lo + LANES] = skip_part + jnp.where(
            first, 0.0, skip_out[0:1, lo : lo + LANES]
        )
        tv = (sv * fall_pair).astype(BF)
        grown_low = grown.astype(BF)
        dwritten = dwritten + mm_nt(tv, after_low[:, lo : lo + LANES])
        dreadout = dreadout + mm_nt_exact(grown, before[:, lo : lo + LANES])
        dstate[:, lo : lo + LANES] = jnp.exp(last_pair) * after[
            :, lo : lo + LANES
        ] + mm(readout_t, grown_low)
    low_top = dscores[:HALF, :].astype(BF)
    low_bottom = dscores[HALF:, HALF:].astype(BF)
    gbuf[:HALF, lanes_v : lanes_v + N] = dwritten[:HALF] + mm(low_top, readout)
    gbuf[HALF:, lanes_v : lanes_v + N] = dwritten[HALF:] + mm(low_bottom, readout[HALF:])
    turned_left = dscores[:HALF, :HALF].T.astype(BF)
    turned_right = dscores[:HALF, HALF:].T.astype(BF)
    turned_low = dscores[HALF:, HALF:].T.astype(BF)
    gbuf[:HALF, lanes_v + N :] = dreadout[:HALF] + mm(turned_left, written[:HALF])
    gbuf[HALF:, lanes_v + N :] = (
        dreadout[HALF:] + mm(turned_right, written[:HALF]) + mm(turned_low, written[HALF:])
    )

    suffix = row_sums[...].T - col_sums[...] + inner
    grad_a = (
        split_sum(anti, suffix, lanes_v // P_SIZE)
        + split_sum(rows > cols, within, lanes_v // P_SIZE)
        + grow_last * through
    )
    grad_step = direct + rate * grad_a
    grad_raw = grad_step * sigmoid(dtp)
    decay_part = jnp.sum(grad_a * step, axis=0, keepdims=True) * rate
    bias_part = jnp.sum(grad_raw, axis=0, keepdims=True)
    head_row = lax.broadcasted_iota(jnp.int32, (8, LANES), 0)
    head_part = jnp.where(head_row == 0, bias_part, jnp.where(head_row == 1, decay_part, 0.0))

    grad_pre = gbuf[...] * (sig * (1.0 + pre * (1.0 - sig)))
    gext[pl.ds(STRETCH, HALO), :] = jnp.where(next_fresh, 0.0, gext[pl.ds(0, HALO), :])
    gext[pl.ds(0, STRETCH), :] = grad_pre
    grad_in = grad_pre * taps[TAPS - 1 : TAPS, :]
    for j in range(TAPS - 1):
        up = TAPS - 1 - j
        grad_in = grad_in + gext[pl.ds(up, STRETCH), :] * taps[j : j + 1, :]
    conv_row = lax.broadcasted_iota(jnp.int32, (8, lanes_x), 0)
    conv_part = jnp.where(conv_row == TAPS, jnp.sum(grad_pre, axis=0, keepdims=True), 0.0)
    for j in range(TAPS):
        low = HALO - (TAPS - 1) + j
        conv_part = jnp.where(
            conv_row == j,
            jnp.sum(grad_pre * ext[pl.ds(low, STRETCH), :], axis=0, keepdims=True),
            conv_part,
        )
    conv_out[...] = conv_part + jnp.where(first, 0.0, conv_out[...])
    head_out[...] = head_part + jnp.where(first, 0.0, head_out[...])

    grad_in_low = grad_in.astype(BF)
    grad_raw_low = grad_raw.astype(BF)
    f = mm_nt(dgate[...], wg[...])
    f = f + mm_nt(grad_in_low, w1[:, :lanes_x])
    f = f + mm_nt(grad_raw_low, w1[:, lanes_x:])
    f_out[...] = f.astype(BF)
    gpv_out[...] = grad_in_low[:, :lanes_v]
    gps_out[:, : 2 * N] = grad_in_low[:, lanes_v:]
    gps_out[:, 2 * N :] = grad_raw_low


def full(shape):
    return pl.BlockSpec(shape, lambda c, *_: (0,) * len(shape))


def tokens(width):
    return pl.BlockSpec((STRETCH, width), lambda c, *_: (c, 0))


def cost(total, depth, lanes, passes):
    return pl.CostEstimate(
        flops=int(2 * total * depth * lanes * passes), bytes_accessed=0, transcendentals=0
    )


def params(name_limit=VMEM_BYTES):
    return pltpu.CompilerParams(
        dimension_semantics=("arbitrary",), vmem_limit_bytes=name_limit
    )


def spreaders(lanes_v):
    heads_here = lanes_v // P_SIZE
    return spreader(heads_here, P_SIZE), spreader(heads_here, LANES)


def run_forward(starts, hid, gain, w1, taps, heads, skip):
    count, depth = starts.shape[0], hid.shape[1]
    lanes_v, lanes_x = skip.shape[1], taps.shape[1]
    total = hid.shape[0]
    return pl.pallas_call(
        forward_kernel,
        grid_spec=pltpu.PrefetchScalarGridSpec(
            num_scalar_prefetch=1,
            grid=(count,),
            in_specs=[
                tokens(depth),
                full(gain.shape),
                full((depth, w1.shape[1])),
                full(taps.shape),
                full(heads.shape),
                full(skip.shape),
                full((LANES, lanes_v)),
                full((LANES, 2 * lanes_v)),
            ],
            out_specs=[
                tokens(depth),
                tokens(lanes_x),
                tokens(LANES),
                tokens(lanes_v),
                pl.BlockSpec((1, N, lanes_v), lambda c, *_: (c, 0, 0)),
            ],
            scratch_shapes=[
                pltpu.VMEM((N, lanes_v), F32),
                pltpu.VMEM((STRETCH + HALO, lanes_x), F32),
                pltpu.VMEM((STRETCH, STRETCH), F32),
                pltpu.VMEM((2, STRETCH, STRETCH), BF),
                pltpu.VMEM((STRETCH, 2 * lanes_v), F32),
                pltpu.VMEM((STRETCH, lanes_v), F32),
            ],
        ),
        out_shape=[
            jax.ShapeDtypeStruct((total, depth), BF),
            jax.ShapeDtypeStruct((total, lanes_x), F32),
            jax.ShapeDtypeStruct((total, LANES), F32),
            jax.ShapeDtypeStruct((total, lanes_v), F32),
            jax.ShapeDtypeStruct((count, N, lanes_v), F32),
        ],
        compiler_params=params(),
        cost_estimate=cost(total, depth, lanes_v, 6),
    )(starts, hid, gain, w1, taps, heads, skip, *spreaders(lanes_v))


def run_gate(u, wg, ow, mixed, gain):
    depth = u.shape[1]
    total, lanes_v = mixed.shape
    return pl.pallas_call(
        gate_kernel,
        grid=(total // STRETCH,),
        in_specs=[
            tokens(depth),
            full((depth, lanes_v)),
            full((lanes_v, depth)),
            tokens(lanes_v),
            full(gain.shape),
        ],
        out_specs=[
            tokens(depth),
            tokens(lanes_v),
            pl.BlockSpec((8, STRETCH), lambda c, *_: (0, c)),
        ],
        out_shape=[
            jax.ShapeDtypeStruct((total, depth), BF),
            jax.ShapeDtypeStruct((total, lanes_v), F32),
            jax.ShapeDtypeStruct((8, total), F32),
        ],
        compiler_params=params(),
        cost_estimate=cost(total, depth, lanes_v, 1),
    )(u, wg, ow, mixed, gain)


def run_pull(lengths, cot, ow, gate, mixed, gain):
    count, depth = lengths.shape[0], cot.shape[1]
    total, lanes_v = mixed.shape
    return pl.pallas_call(
        pull_kernel,
        grid_spec=pltpu.PrefetchScalarGridSpec(
            num_scalar_prefetch=1,
            grid=(count,),
            in_specs=[
                tokens(depth),
                full((lanes_v, depth)),
                tokens(lanes_v),
                tokens(lanes_v),
                full(gain.shape),
            ],
            out_specs=[tokens(lanes_v), pl.BlockSpec((8, STRETCH), lambda c, *_: (0, c))],
        ),
        out_shape=[
            jax.ShapeDtypeStruct((total, lanes_v), F32),
            jax.ShapeDtypeStruct((8, total), F32),
        ],
        compiler_params=params(),
        cost_estimate=cost(total, depth, lanes_v, 0.01),
    )(lengths, cot, ow, gate, mixed, gain)


def run_gate_back(lengths, place, outer, strided, hid, cot, gate, gg, mixed, stats, gain):
    count, depth = lengths.shape[0], hid.shape[1]
    total, lanes_v = mixed.shape
    lengths = jnp.concatenate([lengths, place[None]])
    blocks = [(depth // outer, lanes_v)] * outer
    blocks += [(lanes_v // outer, depth)] * outer if strided else [(lanes_v, depth)]
    return pl.pallas_call(
        functools.partial(gate_back_kernel, outer),
        grid_spec=pltpu.PrefetchScalarGridSpec(
            num_scalar_prefetch=1,
            grid=(count,),
            in_specs=[
                tokens(depth),
                tokens(depth),
                tokens(lanes_v),
                tokens(lanes_v),
                tokens(lanes_v),
                tokens(LANES),
                full(gain.shape),
            ],
            out_specs=[
                tokens(lanes_v),
                tokens(lanes_v),
                full((1, lanes_v)),
                *[full(shape) for shape in blocks],
            ],
            scratch_shapes=[
                pltpu.VMEM((lanes_v, depth), F32),
                pltpu.VMEM((depth, lanes_v), F32),
            ],
        ),
        out_shape=[
            jax.ShapeDtypeStruct((total, lanes_v), F32),
            jax.ShapeDtypeStruct((total, lanes_v), BF),
            jax.ShapeDtypeStruct((1, lanes_v), F32),
            *[jax.ShapeDtypeStruct(shape, BF) for shape in blocks],
        ],
        compiler_params=params(),
        cost_estimate=cost(total, depth, lanes_v, 0.01),
    )(lengths, hid, cot, gate, gg, mixed, stats, gain)


def run_backward(starts, depth, xin, dtp, dmix, dgate, sin, w1, wg, taps, heads, skip):
    count = starts.shape[0]
    lanes_v, lanes_x = skip.shape[1], taps.shape[1]
    total = xin.shape[0]
    per = STRETCH // HALO
    shape1 = (depth, w1.shape[1])

    def back(width):
        return pl.BlockSpec((STRETCH, width), lambda i, *_: (count - 1 - i, 0))

    return pl.pallas_call(
        backward_kernel,
        grid_spec=pltpu.PrefetchScalarGridSpec(
            num_scalar_prefetch=1,
            grid=(count,),
            in_specs=[
                back(lanes_x),
                pl.BlockSpec(
                    (HALO, lanes_x), lambda i, *_: (jnp.maximum((count - 1 - i) * per - 1, 0), 0)
                ),
                back(LANES),
                back(lanes_v),
                back(lanes_v),
                pl.BlockSpec((1, N, lanes_v), lambda i, *_: (count - 1 - i, 0, 0)),
                full(shape1),
                full((depth, lanes_v)),
                full(taps.shape),
                full(heads.shape),
                full(skip.shape),
                full((LANES, lanes_v)),
                full((LANES, 2 * lanes_v)),
            ],
            out_specs=[
                back(depth),
                back(lanes_v),
                back(2 * N + LANES),
                full((8, lanes_x)),
                full((8, LANES)),
                full((1, lanes_v)),
            ],
            scratch_shapes=[
                pltpu.VMEM((N, lanes_v), F32),
                pltpu.VMEM((STRETCH + HALO, lanes_x), F32),
                pltpu.VMEM((STRETCH + HALO, lanes_x), F32),
                pltpu.VMEM((STRETCH, lanes_x), F32),
                pltpu.VMEM((STRETCH, STRETCH), F32),
                pltpu.VMEM((STRETCH, STRETCH), F32),
                pltpu.VMEM((2, STRETCH, STRETCH), F32),
                pltpu.VMEM((2, STRETCH, STRETCH), BF),
                pltpu.VMEM((LANES, STRETCH), F32),
                pltpu.VMEM((STRETCH, LANES), F32),
                pltpu.VMEM((STRETCH, 2 * lanes_v), F32),
                pltpu.VMEM((STRETCH, lanes_v), F32),
            ],
        ),
        out_shape=[
            jax.ShapeDtypeStruct((total, depth), BF),
            jax.ShapeDtypeStruct((total, lanes_v), BF),
            jax.ShapeDtypeStruct((total, 2 * N + LANES), BF),
            jax.ShapeDtypeStruct((8, lanes_x), F32),
            jax.ShapeDtypeStruct((8, LANES), F32),
            jax.ShapeDtypeStruct((1, lanes_v), F32),
        ],
        compiler_params=params(),
        cost_estimate=cost(total, depth, lanes_v, 0.01),
    )(starts, xin, xin, dtp, dmix, dgate, sin, w1, wg, taps, heads, skip, *spreaders(lanes_v))


def relay_blocks(part, axis, beside=()):
    count, place = lax.axis_size(axis), lax.axis_index(axis)
    got = []
    right, left = part, part
    for k in range(1, count):
        if k >= 2 and k - 2 < len(beside):
            right, left, beside[k - 2] = lax.optimization_barrier((right, left, beside[k - 2]))
        right = lax.ppermute(right, axis, [(i, i + 1) for i in range(count - 1)])
        left = lax.ppermute(left, axis, [(i + 1, i) for i in range(count - 1)])
        got.append((right, jnp.where(place >= k, place - k, count)))
        got.append((left, jnp.where(place + k < count, place + k, count)))
    return got


def rotation(block, axis, k):
    count = lax.axis_size(axis)
    return lax.ppermute(block, axis, [(i, (i + k) % count) for i in range(count)])


def direct_blocks(part, axis):
    count, place = lax.axis_size(axis), lax.axis_index(axis)
    return [(rotation(part, axis, k), lax.rem(place + count - k, count)) for k in range(1, count)]


def exchanged_sum(blocks, axis):
    total = blocks[0].astype(F32)
    for k in range(1, len(blocks)):
        total = total + rotation(blocks[k], axis, k).astype(F32)
    return total


def assembled(part, got, axis, after=None):
    count, place = lax.axis_size(axis), lax.axis_index(axis)
    rows = part.shape[0]
    start = (0,) * (part.ndim - 1)
    blocks = [part] + [block for block, _ in got]
    places = [place] + [at for _, at in got]
    if after is not None:
        blocks, _ = lax.optimization_barrier((blocks, after))
    whole = jnp.zeros(((count + 1) * rows, *part.shape[1:]), part.dtype)
    for block, at in zip(blocks, places):
        whole = lax.dynamic_update_slice(whole, block, (at * rows, *start))
    return whole


def rows_kernel(outer_h, gate, values, shared, weight, gain, grad_out, norm_out):
    inner, rows, lanes_v = gate.shape
    width = lanes_v // outer_h
    per = lanes_v // P_SIZE // outer_h
    total = jnp.zeros((rows, 1), F32)

    def put(low, part):
        grad_out[:, low : low + part.shape[1]] = part
        old = weight[:, low : low + part.shape[1]].astype(F32)
        return jnp.sum(old * part, axis=1, keepdims=True)

    for base, got in ((0, gate), (DI, values)):
        for f in range(inner):
            for z in range(outer_h):
                part = got[f, :, z * width : (z + 1) * width].astype(F32)
                total = total + put(base + (z * inner + f) * width, part)
    common = jnp.zeros((rows, 2 * N), F32)
    steps = jnp.zeros((rows, H), F32)
    source = lax.broadcasted_iota(jnp.int32, (LANES, H), 0)
    target = lax.broadcasted_iota(jnp.int32, (LANES, H), 1)
    for f in range(inner):
        common = common + shared[f, :, : 2 * N].astype(F32)
        spot = ((source // per) * inner + f) * per + source % per
        chosen = jnp.logical_and(spot == target, source < per * outer_h)
        steps = steps + mm(shared[f, :, 2 * N :], chosen.astype(F32).astype(BF))
    total = total + put(2 * DI, common) + put(2 * DI + 2 * N, steps)
    norm_out[...] = jnp.broadcast_to(total / gain[...], norm_out.shape)


def run_rows(outer_h, gate, values, shared, weight, gain):
    rows, width = weight.shape
    return pl.pallas_call(
        functools.partial(rows_kernel, outer_h),
        out_shape=[
            jax.ShapeDtypeStruct((rows, width), F32),
            jax.ShapeDtypeStruct((rows, LANES), F32),
        ],
        compiler_params=pltpu.CompilerParams(vmem_limit_bytes=VMEM_BYTES),
    )(gate, values, shared, weight, gain)


def body(
    hidden,
    out_cotangent,
    norm_gain,
    in_weight,
    conv_weight,
    conv_bias,
    step_bias,
    decay_log,
    skip_gain,
    gate_gain,
    out_weight,
    stretch_len,
    stretch_start,
):
    outer, inner = lax.axis_size("dp"), lax.axis_size("fsdp")
    place = lax.axis_index("fsdp")
    local_heads = H // inner
    lanes_v = local_heads * P_SIZE
    lanes_x = lanes_v + 2 * N
    rows_w = in_weight.shape[0]
    rows_o = out_weight.shape[0]
    depth = hidden.shape[1]
    strided = rows_o % P_SIZE == 0
    outer_h = outer if strided else 1

    def by_place(whole, axis, unit):
        shape = whole.shape
        cut = (*shape[:axis], outer_h, inner, local_heads // outer_h * unit, *shape[axis + 1 :])
        parts = jnp.moveaxis(whole.reshape(cut), axis + 1, 0)
        return parts.reshape(inner, *shape[:axis], local_heads * unit, *shape[axis + 1 :])

    def from_places(parts, axis, unit):
        shape = parts.shape[1:]
        cut = (inner, *shape[:axis], outer_h, local_heads // outer_h * unit, *shape[axis + 1 :])
        whole = jnp.moveaxis(parts.reshape(cut), 0, axis + 1)
        return whole.reshape(*shape[:axis], H * unit, *shape[axis + 1 :])

    def own(whole, axis, unit):
        return lax.dynamic_index_in_dim(by_place(whole, axis, unit), place, 0, False)

    wide = CONV - 2 * N
    to_values = by_place(in_weight[:, DI : DI + wide], 1, P_SIZE)
    to_shared = jnp.broadcast_to(
        in_weight[None, :, DI + wide : DI + CONV], (inner, rows_w, 2 * N)
    )
    to_steps = by_place(in_weight[:, DI + CONV :], 1, 1)
    to_steps = jnp.pad(to_steps, ((0, 0), (0, 0), (0, LANES - local_heads)))
    sent = jnp.concatenate([to_values, to_shared, to_steps], axis=2)
    w1 = lax.all_to_all(sent, "fsdp", 0, 0, tiled=True).reshape(inner * rows_w, lanes_x + LANES)
    to_gate = by_place(in_weight[:, :DI], 1, P_SIZE)
    wg = lax.all_to_all(to_gate, "fsdp", 0, 0, tiled=True).reshape(inner * rows_w, lanes_v)
    hid = lax.all_gather(hidden, "fsdp", axis=0, tiled=True)

    small = (
        norm_gain,
        gate_gain,
        conv_weight,
        conv_bias,
        step_bias,
        decay_log,
        skip_gain,
        stretch_len.astype(BF),
        stretch_start.astype(BF),
    )
    sizes = [math.prod(a.shape) for a in small]
    packed = jnp.concatenate([a.reshape(-1) for a in small]).astype(F32)
    spread = lax.all_gather(packed[None, None, :], "fsdp", axis=0, tiled=True)[:, 0]
    gains = lax.all_gather(spread[None, :, : sizes[0] + sizes[1]], "dp", axis=0, tiled=True)
    beside = [spread, gains]
    w1_got = relay_blocks(w1, "dp", beside)
    spread, gains = beside
    if strided:
        ow_got = relay_blocks(out_weight, "dp")
        w1, ow_got, wg = lax.optimization_barrier((w1, ow_got, wg))
    w1 = assembled(w1, w1_got, "dp")
    late = max(len(w1_got) - 4, 0)
    wg, _ = lax.optimization_barrier((wg, w1_got[late : late + 2]))
    wg_got = direct_blocks(wg, "dp")
    ends = [sum(sizes[: i + 1]) for i in range(len(sizes))]
    pieces = [spread[:, end - size : end] for end, size in zip(ends, sizes)]
    norm_full = gains[:, :, : sizes[0]].reshape(-1)
    gate_full = gains[:, :, sizes[0] :].reshape(-1)
    conv_full = pieces[2].reshape(CONV, TAPS)
    bias_full = pieces[3].reshape(CONV)
    per_head = [own(a.reshape(H), 0, 1) for a in pieces[4:7]]
    lengths = pieces[7].reshape(-1).astype(jnp.int32)
    starts = pieces[8].reshape(-1).astype(jnp.int32)

    gain_own = own(gate_full, 0, P_SIZE)[None, :]
    taps_all = jnp.concatenate([conv_full.T, bias_full[None, :]], axis=0)
    taps = jnp.concatenate([own(taps_all[:, :wide], 1, P_SIZE), taps_all[:, wide:]], axis=1)
    taps = jnp.pad(taps, ((0, 8 - (TAPS + 1)), (0, 0)))
    heads = jnp.stack([per_head[0], -jnp.exp(per_head[1])])
    heads = jnp.pad(heads, ((0, 6), (0, LANES - local_heads)))
    skip = jnp.repeat(per_head[2], P_SIZE)[None, :]

    u, xin, dtp, mixed, sin = run_forward(starts, hid, norm_full[None, :], w1, taps, heads, skip)

    wg = assembled(wg, wg_got, "dp", mixed)
    if strided:
        ow = assembled(out_weight, ow_got, "dp")
    else:
        ow = own(lax.all_gather(out_weight, ("dp", "fsdp"), axis=0, tiled=True), 0, P_SIZE)
    cot, _ = lax.optimization_barrier((out_cotangent, w1))
    cot = lax.all_gather(cot, "fsdp", axis=0, tiled=True)

    branch, gate, squares = run_gate(u, wg, ow, mixed, gain_own)
    gg, along = run_pull(lengths, cot, ow, gate, mixed, gain_own)
    stats = lax.psum(jnp.concatenate([squares[0:1], along[0:1]], axis=0), "fsdp")
    r = lax.rsqrt(stats[0] / DI + EPSILON)
    m = r * stats[1] / DI
    table = jnp.pad(jnp.stack([r, m], axis=1), ((0, 0), (0, LANES - 2)))
    branch = lax.psum_scatter(branch, "fsdp", scatter_dimension=0, tiled=True)

    dmix, dgate, ggg, *blocks = run_gate_back(
        lengths, lax.axis_index("dp"), outer, strided, u, cot, gate, gg, mixed, table, gain_own
    )
    iwg_gate = exchanged_sum(blocks[:outer], "dp").astype(BF)
    if strided:
        out_weight_grad = exchanged_sum(blocks[outer:], "dp")
    else:
        rows = lax.dynamic_update_slice_in_dim(
            jnp.zeros((DI, depth), BF), blocks[outer], place * lanes_v, 0
        )
        out_weight_grad = lax.psum_scatter(rows, ("dp", "fsdp"), scatter_dimension=0, tiled=True)
        out_weight_grad = out_weight_grad.astype(F32)

    def to_rows(mine):
        mine = mine.reshape(inner, rows_w, mine.shape[1])
        return lax.all_to_all(mine, "fsdp", 0, 0, tiled=True)


    f, gpv, gps, conv_sums, head_sums, skip_sums = run_backward(
        starts, depth, xin, dtp, dmix, dgate, sin, w1, wg, taps, heads, skip
    )
    f, branch, out_weight_grad, iwg_gate = lax.optimization_barrier(
        (f, branch, out_weight_grad, iwg_gate)
    )
    f = lax.psum_scatter(f, "fsdp", scatter_dimension=0, tiled=True).astype(F32)
    def by_rows(grad):
        rows = depth // outer
        place_z = lax.axis_index("dp")
        blocks = [
            lax.dynamic_slice_in_dim(grad, lax.rem(place_z + k, outer) * rows, rows, 0)
            for k in range(outer)
        ]
        return exchanged_sum(blocks, "dp").astype(BF)

    iwg_values = by_rows(mm_tn(u, gpv).astype(BF))
    iwg_shared = by_rows(mm_tn(u, gps).astype(BF))
    gate_rows, value_rows, shared_rows = (to_rows(a) for a in (iwg_gate, iwg_values, iwg_shared))
    in_weight_grad, norm_rows = run_rows(
        outer_h, gate_rows, value_rows, shared_rows, in_weight, norm_gain.astype(F32)[:, None]
    )
    norm_gain_grad = norm_rows[:, 0]

    total = hidden.shape[0]
    r_own = lax.dynamic_slice_in_dim(r, place * total, total, 0)
    len_here = jnp.repeat(stretch_len, STRETCH)
    alive = (jnp.arange(total) % STRETCH < len_here).astype(F32)
    rows_float = hidden.astype(F32)
    rs_own = lax.rsqrt(jnp.mean(rows_float * rows_float, axis=1, keepdims=True) + EPSILON)
    block_out = (rows_float + (alive * r_own)[:, None] * branch.astype(F32)).astype(BF)
    unit = rows_float * rs_own
    scaled = f * norm_full[None, :]
    hidden_grad = out_cotangent.astype(F32) + rs_own * (
        scaled - unit * jnp.mean(scaled * unit, axis=1, keepdims=True)
    )

    skip_part = jnp.sum(skip_sums.reshape(local_heads, P_SIZE), axis=1)
    parts = (
        conv_sums[: TAPS + 1, :lanes_v].reshape(-1),
        conv_sums[: TAPS + 1, lanes_v:].reshape(-1),
        head_sums[0:2, :local_heads].reshape(-1),
        skip_part,
        ggg.reshape(-1),
    )
    counts = [a.shape[0] for a in parts]
    bundle = lax.psum(jnp.concatenate(parts), "dp")
    bundle = lax.all_gather(bundle, "fsdp", axis=0, tiled=False)
    stops = [sum(counts[: i + 1]) for i in range(len(counts))]
    cuts = [bundle[:, stop - size : stop] for stop, size in zip(stops, counts)]
    conv_values = from_places(cuts[0].reshape(inner, TAPS + 1, lanes_v), 1, P_SIZE)
    conv_shared = jnp.sum(cuts[1].reshape(inner, TAPS + 1, 2 * N), axis=0)
    conv_all = jnp.concatenate([conv_values, conv_shared], axis=1)
    conv_mine = lax.dynamic_slice_in_dim(
        conv_all, place * conv_weight.shape[0], conv_weight.shape[0], 1
    )
    conv_weight_grad = conv_mine[:TAPS].T
    conv_bias_grad = conv_mine[TAPS]

    def heads_mine(parts_h, size):
        whole = from_places(parts_h, 0, 1)
        return lax.dynamic_slice_in_dim(whole, place * size, size, 0)

    pair_sums = cuts[2].reshape(inner, 2, local_heads)
    step_bias_grad = heads_mine(pair_sums[:, 0], step_bias.shape[0])
    decay_log_grad = heads_mine(pair_sums[:, 1], decay_log.shape[0])
    skip_gain_grad = heads_mine(cuts[3], skip_gain.shape[0])
    gate_all = from_places(cuts[4], 0, P_SIZE)
    flat = lax.axis_index("dp") * inner + place
    gate_gain_grad = lax.dynamic_slice_in_dim(
        gate_all, flat * gate_gain.shape[0], gate_gain.shape[0], 0
    )
    return (
        block_out,
        hidden_grad,
        norm_gain_grad,
        in_weight_grad,
        conv_weight_grad,
        conv_bias_grad,
        step_bias_grad,
        decay_log_grad,
        skip_gain_grad,
        gate_gain_grad,
        out_weight_grad,
    )


def solution(mesh):
    both = P(("dp", "fsdp"))
    rows = P(("dp", "fsdp"), None)
    one = P("fsdp")
    return jax.shard_map(
        body,
        mesh=mesh,
        in_specs=(rows, rows, both, rows, P("fsdp", None), one, one, one, one, both, rows, both, both),
        out_specs=(rows, rows, both, rows, P("fsdp", None), one, one, one, one, both, rows),
        check_vma=False,
    )
```

time: 3240 us -> 701 us (0.22)
  waiting for transfers between devices: 1820 us -> 60.6 us
  local copies, waits for them, and re-layouts: 560 us -> 82.5 us
  matrix products: 443 us -> 28.5 us
  Pallas kernels: 0 us -> 273 us
  other arithmetic: 200 us -> 20.6 us
  starting transfers between devices: 5.65 us -> 97.9 us
  blocking collectives: 150 us -> 110 us
    reduce_scatter x2, waiting for transfers between devices: 977 us -> 0.01 us  [the longest x1 0.01 us: body(): branch = lax.psum_scatter(branch, 'fsdp', scatter_dimension=0, tiled=True)]
    all_gather x6 -> x2, waiting for transfers between devices: 840 us -> 0.02 us  [the longest x1 0.02 us: body(): cot = lax.all_gather(cot, 'fsdp', axis=0, tiled=True)]
    dot_general x40 -> x2, matrix products: 443 us -> 28.5 us  [mm_tn(): lax.dot_general(a, b, (((0,), (0,)), ((), ())), preferred_element_type=F32)]
    dynamic_update_slice x20 -> x18, local copies, waits for them, and re-layouts: 368 us -> 24.1 us  [assembled(): whole = lax.dynamic_update_slice(whole, block, (at * rows, *start))]
    pallas_call x0 -> x6, Pallas kernels: none -> 273 us  [the longest x1 106 us: run_backward(): pl.pallas_call(backward_kernel, grid_spec=pltpu.PrefetchScalarGridSpec(nu...]
    ppermute x2 -> x27, starting transfers between devices: 5.29 us -> 75.7 us  [the longest x15 37.9 us: rotation(): lax.ppermute(block, axis, [(i, (i + k) % count) for i in range(count)])]
    reduce_sum x12 -> x4, other arithmetic: 59.9 us -> 4.8 us  [the longest x1 2.67 us: body(): jnp.mean(scaled * unit, axis=1, keepdims=True)]
    ppermute x2 -> x27, waiting for transfers between devices: 0.01 us -> 46.6 us  [the longest x6 34.9 us: relay_blocks(): right = lax.ppermute(right, axis, [(i, i + 1) for i in range(count - 1)])]
  transfers between devices with their start and end apart: 11 -> 35, of which waited for: 7 -> 8; matrix products, arithmetic and copies ran while one was open for 20% -> 17% of each run, Pallas kernels for 0% -> 40%
where the time goes in v1:
time: 701 us; the launch traced here: 688 us
  Pallas kernels  273 us (39%)
  blocking collectives  110 us (16%)
  starting transfers between devices  97.9 us (14%)
  local copies, waits for them, and re-layouts  82.5 us (12%)
  waiting for transfers between devices  60.6 us (9%)
  matrix products  28.5 us (4%)
  other arithmetic  20.6 us (3%)
  between operations  15.1 us (2%)
    pallas_call x1, Pallas kernels, run_backward(): pl.pallas_call(backward_kernel, grid_spec=pltpu.PrefetchScalarGridSpec(nu...  106 us
    pallas_call x1, Pallas kernels, run_forward(): pl.pallas_call(forward_kernel, grid_spec=pltpu.PrefetchScalarGridSpec(num...  61.6 us
    pallas_call x1, Pallas kernels, run_gate_back(): pl.pallas_call(functools.partial(gate_back_kernel, outer), grid_spec=pltp...  45.1 us
    ppermute x15, starting transfers between devices, rotation(): lax.ppermute(block, axis, [(i, (i + k) % count) for i in range(count)])  37.9 us
    ppermute x6, waiting for transfers between devices, relay_blocks(): right = lax.ppermute(right, axis, [(i, i + 1) for i in range(count - 1)])  34.9 us
    psum x1, blocking collectives, body(): bundle = lax.psum(jnp.concatenate(parts), 'dp')  31.1 us
    ppermute x6, starting transfers between devices, relay_blocks(): left = lax.ppermute(left, axis, [(i + 1, i) for i in range(count - 1)])  30.1 us
    pallas_call x1, Pallas kernels, run_gate(): pl.pallas_call(gate_kernel, grid=(total // STRETCH,), in_specs=[tokens(de...  29.9 us
  transfers between devices with their start and end apart: 35, of which 8 were waited for; matrix products, arithmetic and copies ran while one was open for 17% of the time, Pallas kernels for 40%

profile of v1, /device:TPU:30, one launch (start us, length us, event | category | flops | bytes accessed | tf_op | source)
XLA Modules:
  0.0 688.0 jit_solution(9644913836239544368)
XLA Ops:
  11.0 20.8 %all_to_all.25 = bf16[8,64,896]{2,1,0:T(8,128)(2,1)S(1)} all-to-all(bf16[8,64,896]{2,1,0:T(8,128)(2,1)S(1)} %fusion.9), channel_id=1, replica_groups=mesh['dp'=4,'fsdp'=8] {'fsdp'}, dimensions={0} | all-to-all | bytes 1835008 | tf_op jit(solution)/shard_map/all_to_all | solution.py:875
  36.7 6.0 collective-permute-start.5
  43.4 9.2 %all_gather.18 = f32[8,1,2940]{2,1,0:T(1,128)S(1)} all-gather(f32[1,1,2940]{2,1,0:T(1,128)S(1)} %convert_element_type.117), channel_id=1, replica_groups=mesh['dp'=4,'fsdp'=8] {'fsdp'}, dimensions={0}, use_global_device_ids=true | all-gather | bytes 105840 | tf_op jit(solution)/shard_map/all_gather | solution.py:893
  54.8 4.6 collective-permute-done
  60.7 5.5 collective-permute-start.3
  66.2 4.4 collective-permute-done.4
  71.9 5.3 collective-permute-start.7
  77.3 22.1 %collective-permute-done.6 = bf16[128,2048]{1,0:T(8,128)(2,1)} collective-permute-done((bf16[128,2048]{1,0:T(8,128)(2,1)}, bf16[128,2048]{1,0:T(8,128)(2,1)}, u32[]{:S(2)}, u32[]{:S(2)}) %collective-permute-start.6) | collective-permute-done | bytes 524320 | tf_op jit(solution)/shard_map/ppermute | solution.py:747
  100.7 5.4 collective-permute-start.9
  107.4 5.4 all-to-all-start.1
  112.8 13.1 %all-gather = f32[32,192]{1,0:T(8,128)S(1)} all-gather(f32[8,192]{1,0:T(8,128)S(1)} %slice.132), channel_id=2, replica_groups=mesh['dp'=4,'fsdp'=8] {'dp'}, dimensions={0}, use_global_device_ids=true | all-gather | bytes 30720 | tf_op jit(solution)/shard_map/all_gather | solution.py:894
  127.3 5.5 collective-permute-start.11
  143.8 3.8 collective-permute-done.10
  163.3 3.7 reshape.314
  176.2 61.6 %shard_map.248 = (bf16[4096,2048]{1,0:T(8,128)(2,1)}, f32[4096,768]{1,0:T(8,128)}, f32[4096,128]{1,0:T(8,128)}, f32[4096,512]{1,0:T(8,128)}, f32[16,128,512]{2,1,0:T(8,128)}) custom-call(s32[16]{0:T(128)} %convert_element_type.119.starts, bf16[4096,2048]{1,0:T(8,128)(2,1)} %all-gather.5.cloned.1.call-done.hid, f32[1,2048]{1,0:T(1,128)} %broadcast_in_dim_reshape.10.gain, ...), custom_call_target="tpu_custom_call" | custom-call | flops 51539607552 | tf_op jit(solution)/shard_map/pallas_call | solution.py:533
  242.9 29.9 %shard_map.249 = (bf16[4096,2048]{1,0:T(8,128)(2,1)}, f32[4096,512]{1,0:T(8,128)}, f32[8,4096]{1,0:T(8,128)}) custom-call(bf16[4096,2048]{1,0:T(8,128)(2,1)} %get-tuple-element.77.u.hid, bf16[2560,512]{1,0:T(8,128)(2,1)} %copy-done.1, bf16[640,2048]{1,0:T(8,128)(2,1)} %copy-done.2, f32[4096,512]{1,0:T(8,128)} %get-tuple-element.80.mixed, ...), custom_call_target="tpu_custom_call" | custom-call | flops 8589934592 | tf_op jit(solution)/shard_map/pallas_call | solution.py:579
  274.6 27.5 %shard_map.250 = (f32[4096,512]{1,0:T(8,128)}, f32[8,4096]{1,0:T(8,128)}) custom-call(s32[16]{0:T(128)} %copy-done.18, bf16[4096,2048]{1,0:T(8,128)(2,1)} %all-gather.7.cloned.1.call-done.cot, bf16[640,2048]{1,0:T(8,128)(2,1)} %copy-done.2, f32[4096,512]{1,0:T(8,128)} %get-tuple-element.99.gate, f32[4096,512]{1,0:T(8,128)} %get-tuple-element.80.mixed, ...), custom_call_target="tpu_custom_call" | custom-call | flops 85899344 | tf_op jit(solution)/shard_map/pallas_call | solution.py:607
  303.0 20.2 %psum.14 = f32[2,4096]{1,0:T(2,128)S(1)} all-reduce(f32[2,4096]{1,0:T(2,128)S(1)} %pad_maximum_fusion), channel_id=1, replica_groups=mesh['dp'=4,'fsdp'=8] {'fsdp'}, use_global_device_ids=true, to_apply=%region_0.1 | all-reduce | flops 8192 | bytes 65536 | tf_op jit(solution)/shard_map/psum | solution.py:935
  325.4 45.1 %shard_map.251 = (f32[4096,512]{1,0:T(8,128)}, bf16[4096,512]{1,0:T(8,128)(2,1)}, f32[1,512]{1,0:T(1,128)}, bf16[512,512]{1,0:T(8,128)(2,1)}, bf16[512,512]{1,0:...) custom-call(s32[17]{0:T(128)} %pad_add_fusion.lengths, ...), custom_call_target="tpu_custom_call" | custom-call | flops 85899344 | tf_op jit(solution)/shard_map/pallas_call | solution.py:636
  377.0 9.5 %collective-permute-done.18 = bf16[512,512]{1,0:T(8,128)(2,1)S(1)} collective-permute-done((bf16[512,512]{1,0:T(8,128)(2,1)}, bf16[512,512]{1,0:T(8,128)(2,1)S(1)}, u32[]{:S(2)}, u32[]{:S(2)}) %collective-permute-start.18) | collective-permute-done | bytes 524320 | tf_op jit(solution)/shard_map/ppermute | solution.py:756
  386.5 22.8 %collective-permute-start.17 = (bf16[128,2048]{1,0:T(8,128)(2,1)}, bf16[128,2048]{1,0:T(8,128)(2,1)S(1)}, u32[]{:S(2)}, u32[]{:S(2)}) collective-permute-start(bf16[128,2048]{1,0:T(8,128)(2,1)} %get-tuple-element.112), channel_id=1, source_target_pairs={{0,24},{8,0},{16,8},{24,16},{1,25},{9,1},{17,9},{25,17},{2,26},{10... | collective-permute-start | bytes 1572872 | tf_op jit(solution)/shard_map/ppermute | solution.py:756
  409.3 105.6 %shard_map.252 = (bf16[4096,2048]{1,0:T(8,128)(2,1)}, bf16[4096,512]{1,0:T(8,128)(2,1)}, bf16[4096,384]{1,0:T(8,128)(2,1)}, f32[8,768]{1,0:T(8,128)}, f32[8,128]{1,0:T(8,128)}, /*index=5*/f32[1,512]{1,0:T(1,128)}) custom-call(s32[16]{0:T(128)} %convert_element_type.119.starts, f32[4096,768]{1,0:T(8,128)} %get-tuple-element.101.xin.xprev, ...), custom_call_target="tpu_custom_call" | custom-call | flops 85899344 | tf_op jit(solution)/shard_map/pallas_call | solution.py:682
  520.6 13.5 %convolution_convert_fusion.1 = bf16[2048,384]{1,0:T(8,128)(2,1)S(1)} fusion(bf16[4096,2048]{1,0:T(8,128)(2,1)} %get-tuple-element.77.u.hid, bf16[4096,384]{1,0:T(8,128)(2,1)} %get-tuple-element.121), kind=kOutput, calls=%fused_computation.13 | convolution fusion | flops 6443237376 | bytes 21495808 | tf_op jit(solution)/shard_map/dot_general | solution.py:41
  538.5 15.0 %convolution_convert_fusion = bf16[2048,512]{1,0:T(8,128)(2,1)} fusion(bf16[4096,2048]{1,0:T(8,128)(2,1)} %get-tuple-element.77.u.hid, bf16[4096,512]{1,0:T(8,128)(2,1)S(1)} %copy-done.29), kind=kOutput, calls=%fused_computation.12 | convolution fusion | flops 8590983168 | bytes 23068672 | tf_op jit(solution)/shard_map/dot_general | solution.py:41
  560.8 31.1 %psum.15 = f32[1,4376]{1,0:T(1,128)S(1)} all-reduce(f32[1,4376]{1,0:T(1,128)S(1)} %all_gather.22), channel_id=1, replica_groups=mesh['dp'=4,'fsdp'=8] {'dp'}, use_global_device_ids=true, to_apply=%region_6.7 | all-reduce | flops 4376 | bytes 35008 | tf_op jit(solution)/shard_map/psum | solution.py:1005
  592.1 14.9 %all-gather.1 = f32[8,1,4376]{2,1,0:T(1,128)S(1)} all-gather(f32[1,1,4376]{2,1,0:T(1,128)S(1)} %bitcast.136), channel_id=1, replica_groups=mesh['dp'=4,'fsdp'=8] {'fsdp'}, dimensions={0}, use_global_device_ids=true | all-gather | bytes 157536 | tf_op jit(solution)/shard_map/all_gather | solution.py:1006
  615.1 5.0 all-to-all-start.4
  622.8 7.8 %all-to-all-done.4.shared = bf16[8,64,384]{2,1,0:T(8,128)(2,1)S(1)} async-done(((bf16[8,64,384]{2,1,0:T(8,128)(2,1)}), bf16[8,64,384]{2,1,0:T(8,128)(2,1)S(1)}, u32[]{:S(2)}, u32[]{:S(2)}) %all-to-all-start.4) | async-done | bytes 393248 | tf_op jit(solution)/shard_map/all_to_all | solution.py:956
  630.6 5.8 all-to-all-start.3
  638.3 5.5 all-to-all-done.3.values
  643.8 5.8 all-to-all-start.2
  676.1 4.9 fusion.5
  (257 shorter events, 126.3 us)
Async XLA Ops:
  7.2 169.0 %all-gather.5.cloned.1.call-start = ((), (), s32[]{:S(2)}) async-start(), calls=%async_computation.7 | async-start | bytes 18874368 | tf_op jit(solution)/shard_map/all_gather | solution.py:878
  31.8 23.0 %collective-permute-start.1 = (bf16[512,896]{1,0:T(8,128)(2,1)S(1)}, bf16[512,896]{1,0:T(8,128)(2,1)S(1)}, u32[]{:S(2)}, u32[]{:S(2)}) collective-permute-start(bf16[512,896]{1,0:T(8,128)(2,1)S(1)} %bitcast.113), channel_id=1, source_target_pairs={{8,0},{16,8},{24,16},{9,1},{17,9},{25,17},{10,2},{18,10},{26,18},{... | collective-permute-start | bytes 2752520 | tf_op jit(solution)/shard_map/ppermute | solution.py:748
  34.1 25.3 %collective-permute-start = (bf16[512,896]{1,0:T(8,128)(2,1)S(1)}, bf16[512,896]{1,0:T(8,128)(2,1)}, u32[]{:S(2)}, u32[]{:S(2)}) collective-permute-start(bf16[512,896]{1,0:T(8,128)(2,1)S(1)} %bitcast.114), channel_id=1, source_target_pairs={{0,8},{8,16},{16,24},{1,9},{9,17},{17,25},{2,10},{10,18},{18,26},{... | collective-permute-start | bytes 2752520 | tf_op jit(solution)/shard_map/ppermute | solution.py:747
  35.4 35.2 %collective-permute-start.4 = (bf16[128,2048]{1,0:T(8,128)(2,1)S(1)}, bf16[128,2048]{1,0:T(8,128)(2,1)}, u32[]{:S(2)}, u32[]{:S(2)}) collective-permute-start(bf16[128,2048]{1,0:T(8,128)(2,1)S(1)} %copy-done.10), channel_id=1, source_target_pairs={{0,8},{8,16},{16,24},{1,9},{9,17},{17,25},{2,10},{10,18},{18,26},{... | collective-permute-start | bytes 1572872 | tf_op jit(solution)/shard_map/ppermute | solution.py:747
  36.7 35.2 %collective-permute-start.5 = (bf16[128,2048]{1,0:T(8,128)(2,1)S(1)}, bf16[128,2048]{1,0:T(8,128)(2,1)}, u32[]{:S(2)}, u32[]{:S(2)}) collective-permute-start(bf16[128,2048]{1,0:T(8,128)(2,1)S(1)} %copy-done.10), channel_id=1, source_target_pairs={{8,0},{16,8},{24,16},{9,1},{17,9},{25,17},{10,2},{18,10},{26,18},{... | collective-permute-start | bytes 1572872 | tf_op jit(solution)/shard_map/ppermute | solution.py:748
  59.4 66.6 %collective-permute-start.2 = (bf16[512,896]{1,0:T(8,128)(2,1)}, bf16[512,896]{1,0:T(8,128)(2,1)}, u32[]{:S(2)}, u32[]{:S(2)}) collective-permute-start(bf16[512,896]{1,0:T(8,128)(2,1)} %collective-permute-done), channel_id=1, source_target_pairs={{0,8},{8,16},{16,24},{1,9},{9,17},{17,25},{2,10},{10,18},{18,26},{... | collective-permute-start | bytes 2752520 | tf_op jit(solution)/shard_map/ppermute | solution.py:747
  60.7 65.3 %collective-permute-start.3 = (bf16[512,896]{1,0:T(8,128)(2,1)S(1)}, bf16[512,896]{1,0:T(8,128)(2,1)}, u32[]{:S(2)}, u32[]{:S(2)}) collective-permute-start(bf16[512,896]{1,0:T(8,128)(2,1)S(1)} %collective-permute-done.1), channel_id=1, source_target_pairs={{8,0},{16,8},{24,16},{9,1},{17,9},{25,17},{10,2},{18,10},{26,18},{... | collective-permute-start | bytes 2752520 | tf_op jit(solution)/shard_map/ppermute | solution.py:748
  70.6 28.8 %collective-permute-start.6 = (bf16[128,2048]{1,0:T(8,128)(2,1)}, bf16[128,2048]{1,0:T(8,128)(2,1)}, u32[]{:S(2)}, u32[]{:S(2)}) collective-permute-start(bf16[128,2048]{1,0:T(8,128)(2,1)} %collective-permute-done.4), channel_id=1, source_target_pairs={{0,8},{8,16},{16,24},{1,9},{9,17},{17,25},{2,10},{10,18},{18,26},{... | collective-permute-start | bytes 1572872 | tf_op jit(solution)/shard_map/ppermute | solution.py:747
  71.9 28.7 %collective-permute-start.7 = (bf16[128,2048]{1,0:T(8,128)(2,1)}, bf16[128,2048]{1,0:T(8,128)(2,1)}, u32[]{:S(2)}, u32[]{:S(2)}) collective-permute-start(bf16[128,2048]{1,0:T(8,128)(2,1)} %collective-permute-done.5), channel_id=1, source_target_pairs={{8,0},{16,8},{24,16},{9,1},{17,9},{25,17},{10,2},{18,10},{26,18},{... | collective-permute-start | bytes 1572872 | tf_op jit(solution)/shard_map/ppermute | solution.py:748
  99.4 33.4 %collective-permute-start.8 = (bf16[128,2048]{1,0:T(8,128)(2,1)}, bf16[128,2048]{1,0:T(8,128)(2,1)}, u32[]{:S(2)}, u32[]{:S(2)}) collective-permute-start(bf16[128,2048]{1,0:T(8,128)(2,1)} %collective-permute-done.6), channel_id=1, source_target_pairs={{0,8},{8,16},{16,24},{1,9},{9,17},{17,25},{2,10},{10,18},{18,26},{... | collective-permute-start | bytes 1572872 | tf_op jit(solution)/shard_map/ppermute | solution.py:747
  100.7 32.1 %collective-permute-start.9 = (bf16[128,2048]{1,0:T(8,128)(2,1)}, bf16[128,2048]{1,0:T(8,128)(2,1)}, u32[]{:S(2)}, u32[]{:S(2)}) collective-permute-start(bf16[128,2048]{1,0:T(8,128)(2,1)} %collective-permute-done.7), channel_id=1, source_target_pairs={{8,0},{16,8},{24,16},{9,1},{17,9},{25,17},{10,2},{18,10},{26,18},{... | collective-permute-start | bytes 1572872 | tf_op jit(solution)/shard_map/ppermute | solution.py:748
  107.4 25.4 %all-to-all-start.1 = ((bf16[8,64,512]{2,1,0:T(8,128)(2,1)}), bf16[8,64,512]{2,1,0:T(8,128)(2,1)S(1)}, u32[]{:S(2)}, u32[]{:S(2)}) async-start(bf16[8,64,512]{2,1,0:T(8,128)(2,1)} %reshape.312), calls=%async_computation.1 | async-start | bytes 1048576 | tf_op jit(solution)/shard_map/all_to_all | solution.py:877
  112.8 161.7 %all-gather.7.cloned.1.call-start = ((), (), s32[]{:S(2)}) async-start(), calls=%async_computation.8 | async-start | bytes 18874368 | tf_op jit(solution)/shard_map/all_gather | solution.py:931
  126.0 21.7 %collective-permute-start.10 = (bf16[512,896]{1,0:T(8,128)(2,1)}, bf16[512,896]{1,0:T(8,128)(2,1)}, u32[]{:S(2)}, u32[]{:S(2)}) collective-permute-start(bf16[512,896]{1,0:T(8,128)(2,1)} %collective-permute-done.2), channel_id=1, source_target_pairs={{0,8},{8,16},{16,24},{1,9},{9,17},{17,25},{2,10},{10,18},{18,26},{... | collective-permute-start | bytes 2752520 | tf_op jit(solution)/shard_map/ppermute | solution.py:747
  127.3 22.6 %collective-permute-start.11 = (bf16[512,896]{1,0:T(8,128)(2,1)}, bf16[512,896]{1,0:T(8,128)(2,1)}, u32[]{:S(2)}, u32[]{:S(2)}) collective-permute-start(bf16[512,896]{1,0:T(8,128)(2,1)} %collective-permute-done.3), channel_id=1, source_target_pairs={{8,0},{16,8},{24,16},{9,1},{17,9},{25,17},{10,2},{18,10},{26,18},{... | collective-permute-start | bytes 2752520 | tf_op jit(solution)/shard_map/ppermute | solution.py:748
  152.1 365.2 %reduce-scatter.3.cloned.1.call-start = ((), (), s32[]{:S(2)}) async-start(), calls=%async_computation.9 | async-start | bytes 18874368 | tf_op jit(solution)/shard_map/reduce_scatter | solution.py:939
  170.5 67.3 %collective-permute-start.14 = (bf16[512,512]{1,0:T(8,128)(2,1)S(1)}, bf16[512,512]{1,0:T(8,128)(2,1)}, u32[]{:S(2)}, u32[]{:S(2)}) collective-permute-start(bf16[512,512]{1,0:T(8,128)(2,1)S(1)} %bitcast.116), channel_id=1, source_target_pairs={{0,24},{8,0},{16,8},{24,16},{1,25},{9,1},{17,9},{25,17},{2,26},{10... | collective-permute-start | bytes 1572872 | tf_op jit(solution)/shard_map/ppermute | solution.py:756
  172.1 65.7 %collective-permute-start.13 = (bf16[512,512]{1,0:T(8,128)(2,1)S(1)}, bf16[512,512]{1,0:T(8,128)(2,1)}, u32[]{:S(2)}, u32[]{:S(2)}) collective-permute-start(bf16[512,512]{1,0:T(8,128)(2,1)S(1)} %bitcast.117), channel_id=1, source_target_pairs={{0,16},{8,24},{16,0},{24,8},{1,17},{9,25},{17,1},{25,9},{2,18},{10... | collective-permute-start | bytes 1572872 | tf_op jit(solution)/shard_map/ppermute | solution.py:756
  173.6 64.2 %collective-permute-start.12 = (bf16[512,512]{1,0:T(8,128)(2,1)S(1)}, bf16[512,512]{1,0:T(8,128)(2,1)}, u32[]{:S(2)}, u32[]{:S(2)}) collective-permute-start(bf16[512,512]{1,0:T(8,128)(2,1)S(1)} %bitcast.118), channel_id=1, source_target_pairs={{0,8},{8,16},{16,24},{24,0},{1,9},{9,17},{17,25},{25,1},{2,10},{10... | collective-permute-start | bytes 1572872 | tf_op jit(solution)/shard_map/ppermute | solution.py:756
  272.9 400.4 %reduce-scatter.5.cloned.1.call-start = ((), (), s32[]{:S(2)}) async-start(), calls=%async_computation.10 | async-start | bytes 18874368 | tf_op jit(solution)/shard_map/reduce_scatter | solution.py:965
  371.9 143.0 %collective-permute-start.19 = (bf16[512,512]{1,0:T(8,128)(2,1)}, bf16[512,512]{1,0:T(8,128)(2,1)S(1)}, u32[]{:S(2)}, u32[]{:S(2)}) collective-permute-start(bf16[512,512]{1,0:T(8,128)(2,1)} %get-tuple-element.115), channel_id=1, source_target_pairs={{0,16},{8,24},{16,0},{24,8},{1,17},{9,25},{17,1},{25,9},{2,18},{10... | collective-permute-start | bytes 1572872 | tf_op jit(solution)/shard_map/ppermute | solution.py:756
  373.2 141.7 %collective-permute-start.20 = (bf16[512,512]{1,0:T(8,128)(2,1)}, bf16[512,512]{1,0:T(8,128)(2,1)S(1)}, u32[]{:S(2)}, u32[]{:S(2)}) collective-permute-start(bf16[512,512]{1,0:T(8,128)(2,1)} %get-tuple-element.116), channel_id=1, source_target_pairs={{0,24},{8,0},{16,8},{24,16},{1,25},{9,1},{17,9},{25,17},{2,26},{10... | collective-permute-start | bytes 1572872 | tf_op jit(solution)/shard_map/ppermute | solution.py:756
  373.9 142.1 %collective-permute-start.15 = (bf16[128,2048]{1,0:T(8,128)(2,1)}, bf16[128,2048]{1,0:T(8,128)(2,1)S(1)}, u32[]{:S(2)}, u32[]{:S(2)}) collective-permute-start(bf16[128,2048]{1,0:T(8,128)(2,1)} %get-tuple-element.110), channel_id=1, source_target_pairs={{0,8},{8,16},{16,24},{24,0},{1,9},{9,17},{17,25},{25,1},{2,10},{10... | collective-permute-start | bytes 1572872 | tf_op jit(solution)/shard_map/ppermute | solution.py:756
  377.0 138.9 %collective-permute-start.16 = (bf16[128,2048]{1,0:T(8,128)(2,1)}, bf16[128,2048]{1,0:T(8,128)(2,1)S(1)}, u32[]{:S(2)}, u32[]{:S(2)}) collective-permute-start(bf16[128,2048]{1,0:T(8,128)(2,1)} %get-tuple-element.111), channel_id=1, source_target_pairs={{0,16},{8,24},{16,0},{24,8},{1,17},{9,25},{17,1},{25,9},{2,18},{10... | collective-permute-start | bytes 1572872 | tf_op jit(solution)/shard_map/ppermute | solution.py:756
  386.5 129.5 %collective-permute-start.17 = (bf16[128,2048]{1,0:T(8,128)(2,1)}, bf16[128,2048]{1,0:T(8,128)(2,1)S(1)}, u32[]{:S(2)}, u32[]{:S(2)}) collective-permute-start(bf16[128,2048]{1,0:T(8,128)(2,1)} %get-tuple-element.112), channel_id=1, source_target_pairs={{0,24},{8,0},{16,8},{24,16},{1,25},{9,1},{17,9},{25,17},{2,26},{10... | collective-permute-start | bytes 1572872 | tf_op jit(solution)/shard_map/ppermute | solution.py:756
  536.3 55.7 %collective-permute-start.24 = (bf16[512,384]{1,0:T(8,128)(2,1)S(1)}, bf16[512,384]{1,0:T(8,128)(2,1)S(1)}, u32[]{:S(2)}, u32[]{:S(2)}) collective-permute-start(bf16[512,384]{1,0:T(8,128)(2,1)S(1)} %get-tuple-element.136), channel_id=1, source_target_pairs={{0,8},{8,16},{16,24},{24,0},{1,9},{9,17},{17,25},{25,1},{2,10},{10... | collective-permute-start | bytes 1179656 | tf_op jit(solution)/shard_map/ppermute | solution.py:756
  536.3 76.5 %collective-permute-start.26 = (bf16[512,384]{1,0:T(8,128)(2,1)}, bf16[512,384]{1,0:T(8,128)(2,1)}, u32[]{:S(2)}, u32[]{:S(2)}) collective-permute-start(bf16[512,384]{1,0:T(8,128)(2,1)} %get-tuple-element.137), channel_id=1, source_target_pairs={{0,24},{8,0},{16,8},{24,16},{1,25},{9,1},{17,9},{25,17},{2,26},{10... | collective-permute-start | bytes 1179656 | tf_op jit(solution)/shard_map/ppermute | solution.py:756
  538.5 74.3 %collective-permute-start.25 = (bf16[512,384]{1,0:T(8,128)(2,1)}, bf16[512,384]{1,0:T(8,128)(2,1)}, u32[]{:S(2)}, u32[]{:S(2)}) collective-permute-start(bf16[512,384]{1,0:T(8,128)(2,1)} %get-tuple-element.138), channel_id=1, source_target_pairs={{0,16},{8,24},{16,0},{24,8},{1,17},{9,25},{17,1},{25,9},{2,18},{10... | collective-permute-start | bytes 1179656 | tf_op jit(solution)/shard_map/ppermute | solution.py:756
  558.8 61.4 %collective-permute-start.21 = (bf16[512,512]{1,0:T(8,128)(2,1)}, bf16[512,512]{1,0:T(8,128)(2,1)}, u32[]{:S(2)}, u32[]{:S(2)}) collective-permute-start(bf16[512,512]{1,0:T(8,128)(2,1)} %get-tuple-element.131), channel_id=1, source_target_pairs={{0,8},{8,16},{16,24},{24,0},{1,9},{9,17},{17,25},{25,1},{2,10},{10... | collective-permute-start | bytes 1572872 | tf_op jit(solution)/shard_map/ppermute | solution.py:756
  560.8 59.4 %collective-permute-start.23 = (bf16[512,512]{1,0:T(8,128)(2,1)}, bf16[512,512]{1,0:T(8,128)(2,1)}, u32[]{:S(2)}, u32[]{:S(2)}) collective-permute-start(bf16[512,512]{1,0:T(8,128)(2,1)} %get-tuple-element.132), channel_id=1, source_target_pairs={{0,24},{8,0},{16,8},{24,16},{1,25},{9,1},{17,9},{25,17},{2,26},{10... | collective-permute-start | bytes 1572872 | tf_op jit(solution)/shard_map/ppermute | solution.py:756
  592.0 28.2 %collective-permute-start.22 = (bf16[512,512]{1,0:T(8,128)(2,1)}, bf16[512,512]{1,0:T(8,128)(2,1)}, u32[]{:S(2)}, u32[]{:S(2)}) collective-permute-start(bf16[512,512]{1,0:T(8,128)(2,1)} %get-tuple-element.133), channel_id=1, source_target_pairs={{0,16},{8,24},{16,0},{24,8},{1,17},{9,25},{17,1},{25,9},{2,18},{10... | collective-permute-start | bytes 1572872 | tf_op jit(solution)/shard_map/ppermute | solution.py:756
  643.8 23.7 %all-to-all-start.2 = ((bf16[8,64,512]{2,1,0:T(8,128)(2,1)}), bf16[8,64,512]{2,1,0:T(8,128)(2,1)S(1)}, u32[]{:S(2)}, u32[]{:S(2)}) async-start(bf16[8,64,512]{2,1,0:T(8,128)(2,1)} %bitcast.30), calls=%async_computation.4 | async-start | bytes 1048576 | tf_op jit(solution)/shard_map/all_to_all | solution.py:956
  (34 other events, 883.0 us)
Sparse Core Ops, SparseCore 0:
  9.9 94.3 all-gather.4
  152.2 89.8 all-gather.6
  273.0 116.3 reduce-scatter.2
  517.4 123.6 reduce-scatter.4

commit v2 on v1

--- a/solution.py
+++ b/solution.py
@@ -104,27 +104,28 @@
 
 
 def forward_kernel(
-    starts, hid, gain, w1, taps, heads, skip, to_pairs, to_lanes, u_out, xin_out, dtp_out, mixed_out, sin_out, state, ext,
+    starts, hid, gain, wv, ws, taps, heads, skip, to_pairs, to_lanes, u_out, xin_out, dtp_out, mixed_out, sin_out, state, ext,
     scores, mixing, columns, steps,
 ):
     c = pl.program_id(0)
     fresh = starts[c] > 0
     lanes_v = skip.shape[1]
-    lanes_x = taps.shape[1]
     rows_in = hid[...]
     wide = rows_in.astype(F32)
     square = jnp.sum(wide * wide, axis=1, keepdims=True)
     rs = lax.rsqrt(square / rows_in.shape[1] + EPSILON)
     u = (wide * rs * gain[...]).astype(BF)
     u_out[...] = u
-    projected = mm(u, w1[...])
-    conv_input = projected[:, :lanes_x]
-    dtp = projected[:, lanes_x:] + heads[0:1, :]
-    xin_out[...] = conv_input
-    dtp_out[...] = dtp
     halo = ext[pl.ds(STRETCH, HALO), :]
     ext[pl.ds(0, HALO), :] = jnp.where(fresh, 0.0, halo)
-    ext[pl.ds(HALO, STRETCH), :] = conv_input
+    from_values = mm(u, wv[...])
+    from_shared = mm(u, ws[...])
+    dtp = from_shared[:, 2 * N :] + heads[0:1, :]
+    xin_out[:, :lanes_v] = from_values
+    xin_out[:, lanes_v:] = from_shared[:, : 2 * N]
+    dtp_out[...] = dtp
+    ext[pl.ds(HALO, STRETCH), :lanes_v] = from_values
+    ext[pl.ds(HALO, STRETCH), lanes_v:] = from_shared[:, : 2 * N]
     pre = convolved(ext, taps)
     act = pre * sigmoid(pre)
     values = act[:, :lanes_v]
@@ -140,7 +141,7 @@
     scores[...] = mm_nt(readout, written)
     columns[...] = mm(three_parts(decay, lanes_v // P_SIZE), to_lanes[...])
     steps[...] = mm(three_parts(step, lanes_v // P_SIZE), to_pairs[...])
-    carried = mm(readout, before.astype(BF))
+    carried = mm_exact(act[:, lanes_v + N :], before)
     written_t = act[:, lanes_v : lanes_v + N].T.astype(BF)
     left = half_mask(STRETCH)
     for pair in range(lanes_v // LANES):
@@ -282,7 +283,8 @@
     dmix,
     dgate,
     sin,
-    w1,
+    wv,
+    ws,
     wg,
     taps,
     heads,
@@ -493,8 +495,9 @@
     grad_in_low = grad_in.astype(BF)
     grad_raw_low = grad_raw.astype(BF)
     f = mm_nt(dgate[...], wg[...])
-    f = f + mm_nt(grad_in_low, w1[:, :lanes_x])
-    f = f + mm_nt(grad_raw_low, w1[:, lanes_x:])
+    f = f + mm_nt(grad_in_low[:, :lanes_v], wv[...])
+    f = f + mm_nt(grad_in_low[:, lanes_v:], ws[:, : 2 * N])
+    f = f + mm_nt(grad_raw_low, ws[:, 2 * N :])
     f_out[...] = f.astype(BF)
     gpv_out[...] = grad_in_low[:, :lanes_v]
     gps_out[:, : 2 * N] = grad_in_low[:, lanes_v:]
@@ -526,7 +529,7 @@
     return spreader(heads_here, P_SIZE), spreader(heads_here, LANES)
 
 
-def run_forward(starts, hid, gain, w1, taps, heads, skip):
+def run_forward(starts, hid, gain, wv, ws, taps, heads, skip):
     count, depth = starts.shape[0], hid.shape[1]
     lanes_v, lanes_x = skip.shape[1], taps.shape[1]
     total = hid.shape[0]
@@ -538,7 +541,8 @@
             in_specs=[
                 tokens(depth),
                 full(gain.shape),
-                full((depth, w1.shape[1])),
+                full((depth, wv.shape[1])),
+                full((depth, ws.shape[1])),
                 full(taps.shape),
                 full(heads.shape),
                 full(skip.shape),
@@ -570,7 +574,7 @@
         ],
         compiler_params=params(),
         cost_estimate=cost(total, depth, lanes_v, 6),
-    )(starts, hid, gain, w1, taps, heads, skip, *spreaders(lanes_v))
+    )(starts, hid, gain, wv, ws, taps, heads, skip, *spreaders(lanes_v))
 
 
 def run_gate(u, wg, ow, mixed, gain):
@@ -669,12 +673,11 @@
     )(lengths, hid, cot, gate, gg, mixed, stats, gain)
 
 
-def run_backward(starts, depth, xin, dtp, dmix, dgate, sin, w1, wg, taps, heads, skip):
+def run_backward(starts, depth, xin, dtp, dmix, dgate, sin, wv, ws, wg, taps, heads, skip):
     count = starts.shape[0]
     lanes_v, lanes_x = skip.shape[1], taps.shape[1]
     total = xin.shape[0]
     per = STRETCH // HALO
-    shape1 = (depth, w1.shape[1])
 
     def back(width):
         return pl.BlockSpec((STRETCH, width), lambda i, *_: (count - 1 - i, 0))
@@ -693,7 +696,8 @@
                 back(lanes_v),
                 back(lanes_v),
                 pl.BlockSpec((1, N, lanes_v), lambda i, *_: (count - 1 - i, 0, 0)),
-                full(shape1),
+                full((depth, wv.shape[1])),
+                full((depth, ws.shape[1])),
                 full((depth, lanes_v)),
                 full(taps.shape),
                 full(heads.shape),
@@ -734,16 +738,14 @@
         ],
         compiler_params=params(),
         cost_estimate=cost(total, depth, lanes_v, 0.01),
-    )(starts, xin, xin, dtp, dmix, dgate, sin, w1, wg, taps, heads, skip, *spreaders(lanes_v))
-
-
-def relay_blocks(part, axis, beside=()):
+    )(starts, xin, xin, dtp, dmix, dgate, sin, wv, ws, wg, taps, heads, skip, *spreaders(lanes_v))
+
+
+def relay_blocks(part, axis):
     count, place = lax.axis_size(axis), lax.axis_index(axis)
     got = []
     right, left = part, part
     for k in range(1, count):
-        if k >= 2 and k - 2 < len(beside):
-            right, left, beside[k - 2] = lax.optimization_barrier((right, left, beside[k - 2]))
         right = lax.ppermute(right, axis, [(i, i + 1) for i in range(count - 1)])
         left = lax.ppermute(left, axis, [(i + 1, i) for i in range(count - 1)])
         got.append((right, jnp.where(place >= k, place - k, count)))
@@ -865,21 +867,11 @@
         return lax.dynamic_index_in_dim(by_place(whole, axis, unit), place, 0, False)
 
     wide = CONV - 2 * N
-    to_values = by_place(in_weight[:, DI : DI + wide], 1, P_SIZE)
-    to_shared = jnp.broadcast_to(
-        in_weight[None, :, DI + wide : DI + CONV], (inner, rows_w, 2 * N)
-    )
-    to_steps = by_place(in_weight[:, DI + CONV :], 1, 1)
-    to_steps = jnp.pad(to_steps, ((0, 0), (0, 0), (0, LANES - local_heads)))
-    sent = jnp.concatenate([to_values, to_shared, to_steps], axis=2)
-    w1 = lax.all_to_all(sent, "fsdp", 0, 0, tiled=True).reshape(inner * rows_w, lanes_x + LANES)
-    to_gate = by_place(in_weight[:, :DI], 1, P_SIZE)
-    wg = lax.all_to_all(to_gate, "fsdp", 0, 0, tiled=True).reshape(inner * rows_w, lanes_v)
     hid = lax.all_gather(hidden, "fsdp", axis=0, tiled=True)
 
+    shared_width = 2 * N + H
+    gains = (norm_gain, gate_gain)
     small = (
-        norm_gain,
-        gate_gain,
         conv_weight,
         conv_bias,
         step_bias,
@@ -888,29 +880,63 @@
         stretch_len.astype(BF),
         stretch_start.astype(BF),
     )
-    sizes = [math.prod(a.shape) for a in small]
-    packed = jnp.concatenate([a.reshape(-1) for a in small]).astype(F32)
-    spread = lax.all_gather(packed[None, None, :], "fsdp", axis=0, tiled=True)[:, 0]
-    gains = lax.all_gather(spread[None, :, : sizes[0] + sizes[1]], "dp", axis=0, tiled=True)
-    beside = [spread, gains]
-    w1_got = relay_blocks(w1, "dp", beside)
-    spread, gains = beside
+
+    def in_rows(arrays):
+        flat = jnp.concatenate([a.reshape(-1) for a in arrays])
+        rows = -(-flat.shape[0] // shared_width)
+        return jnp.pad(flat, (0, rows * shared_width - flat.shape[0])).reshape(rows, shared_width)
+
+    gain_rows, small_rows = in_rows(gains), in_rows(small)
+    block = jnp.concatenate([in_weight[:, DI + wide :], gain_rows, small_rows], axis=0)
+    height = -(-block.shape[0] // 16) * 16
+    block = jnp.pad(block, ((0, height - block.shape[0]), (0, 0)))
+    along = assembled(block, direct_blocks(block, "dp"), "dp")[: outer * height]
+    along = jnp.broadcast_to(along[None], (inner, *along.shape))
+    common = lax.all_to_all(along, "fsdp", 0, 0, tiled=True)
+    common = common.reshape(inner, outer, height, shared_width)
+
+    wv = lax.all_to_all(by_place(in_weight[:, DI : DI + wide], 1, P_SIZE), "fsdp", 0, 0, tiled=True)
+    wv = wv.reshape(inner * rows_w, lanes_v)
+    wg = lax.all_to_all(by_place(in_weight[:, :DI], 1, P_SIZE), "fsdp", 0, 0, tiled=True)
+    wg = wg.reshape(inner * rows_w, lanes_v)
+    cot, _ = lax.optimization_barrier((out_cotangent, wv))
+    cot = lax.all_gather(cot, "fsdp", axis=0, tiled=True)
+    wv_got = relay_blocks(wv, "dp")
+    late = max(len(wv_got) - 4, 0)
+    wg, ow, _ = lax.optimization_barrier((wg, out_weight, wv_got[late : late + 2]))
+    wg_got = direct_blocks(wg, "dp")
     if strided:
-        ow_got = relay_blocks(out_weight, "dp")
-        w1, ow_got, wg = lax.optimization_barrier((w1, ow_got, wg))
-    w1 = assembled(w1, w1_got, "dp")
-    late = max(len(w1_got) - 4, 0)
-    wg, _ = lax.optimization_barrier((wg, w1_got[late : late + 2]))
-    wg_got = direct_blocks(wg, "dp")
-    ends = [sum(sizes[: i + 1]) for i in range(len(sizes))]
-    pieces = [spread[:, end - size : end] for end, size in zip(ends, sizes)]
-    norm_full = gains[:, :, : sizes[0]].reshape(-1)
-    gate_full = gains[:, :, sizes[0] :].reshape(-1)
-    conv_full = pieces[2].reshape(CONV, TAPS)
-    bias_full = pieces[3].reshape(CONV)
-    per_head = [own(a.reshape(H), 0, 1) for a in pieces[4:7]]
-    lengths = pieces[7].reshape(-1).astype(jnp.int32)
-    starts = pieces[8].reshape(-1).astype(jnp.int32)
+        ow_got = direct_blocks(ow, "dp")
+    wv = assembled(wv, wv_got, "dp")
+
+    rows_all = jnp.swapaxes(common[:, :, :rows_w], 0, 1).reshape(depth, shared_width)
+    head_of = np.arange(H).reshape(outer_h, inner, local_heads // outer_h)
+    order = jnp.asarray(np.swapaxes(head_of, 0, 1).reshape(inner, local_heads))
+    mine = lax.dynamic_index_in_dim(order, place, 0, False)
+    pick = (jnp.arange(H)[:, None] == mine[None, :]).astype(BF)
+    pick = jnp.pad(pick, ((0, 0), (0, LANES - local_heads)))
+    ws = jnp.concatenate([rows_all[:, : 2 * N], mm(rows_all[:, 2 * N :], pick).astype(BF)], axis=1)
+
+    def out_of_rows(rows, arrays):
+        flat = rows.reshape(*rows.shape[:-2], -1).astype(F32)
+        parts, low = [], 0
+        for a in arrays:
+            size = math.prod(a.shape)
+            parts.append(flat[..., low : low + size])
+            low += size
+        return parts
+
+    at = rows_w + gain_rows.shape[0]
+    norm_part, gate_part = out_of_rows(common[:, :, rows_w:at], gains)
+    norm_full = jnp.swapaxes(norm_part, 0, 1).reshape(-1)
+    gate_full = jnp.swapaxes(gate_part, 0, 1).reshape(-1)
+    same = lax.dynamic_index_in_dim(common, lax.axis_index("dp"), 1, False)
+    pieces = out_of_rows(same[:, at : at + small_rows.shape[0]], small)
+    conv_full = pieces[0].reshape(CONV, TAPS)
+    bias_full = pieces[1].reshape(CONV)
+    per_head = [own(a.reshape(H), 0, 1) for a in pieces[2:5]]
+    lengths = pieces[5].reshape(-1).astype(jnp.int32)
+    starts = pieces[6].reshape(-1).astype(jnp.int32)
 
     gain_own = own(gate_full, 0, P_SIZE)[None, :]
     taps_all = jnp.concatenate([conv_full.T, bias_full[None, :]], axis=0)
@@ -920,15 +946,14 @@
     heads = jnp.pad(heads, ((0, 6), (0, LANES - local_heads)))
     skip = jnp.repeat(per_head[2], P_SIZE)[None, :]
 
-    u, xin, dtp, mixed, sin = run_forward(starts, hid, norm_full[None, :], w1, taps, heads, skip)
-
+    u, xin, dtp, mixed, sin = run_forward(
+        starts, hid, norm_full[None, :], wv, ws, taps, heads, skip
+    )
     wg = assembled(wg, wg_got, "dp", mixed)
     if strided:
-        ow = assembled(out_weight, ow_got, "dp")
+        ow = assembled(ow, ow_got, "dp", mixed)
     else:
         ow = own(lax.all_gather(out_weight, ("dp", "fsdp"), axis=0, tiled=True), 0, P_SIZE)
-    cot, _ = lax.optimization_barrier((out_cotangent, w1))
-    cot = lax.all_gather(cot, "fsdp", axis=0, tiled=True)
 
     branch, gate, squares = run_gate(u, wg, ow, mixed, gain_own)
     gg, along = run_pull(lengths, cot, ow, gate, mixed, gain_own)
@@ -957,12 +982,23 @@
 
 
     f, gpv, gps, conv_sums, head_sums, skip_sums = run_backward(
-        starts, depth, xin, dtp, dmix, dgate, sin, w1, wg, taps, heads, skip
-    )
-    f, branch, out_weight_grad, iwg_gate = lax.optimization_barrier(
-        (f, branch, out_weight_grad, iwg_gate)
-    )
-    f = lax.psum_scatter(f, "fsdp", scatter_dimension=0, tiled=True).astype(F32)
+        starts, depth, xin, dtp, dmix, dgate, sin, wv, ws, wg, taps, heads, skip
+    )
+    skip_part = jnp.sum(skip_sums.reshape(local_heads, P_SIZE), axis=1)
+    parts = (
+        conv_sums[: TAPS + 1, :lanes_v].reshape(-1),
+        conv_sums[: TAPS + 1, lanes_v:].reshape(-1),
+        head_sums[0:2, :local_heads].reshape(-1),
+        skip_part,
+        ggg.reshape(-1),
+    )
+    counts = [a.shape[0] for a in parts]
+    bundle = jnp.concatenate(parts)
+    bundle = jnp.pad(bundle, (0, -bundle.shape[0] % (8 * LANES))).reshape(-1, LANES)
+    f, branch, out_weight_grad, iwg_gate, bundle = lax.optimization_barrier(
+        (f, branch, out_weight_grad, iwg_gate, bundle)
+    )
+    f = lax.psum_scatter(f, "fsdp", scatter_dimension=0, tiled=True)
     def by_rows(grad):
         rows = depth // outer
         place_z = lax.axis_index("dp")
@@ -970,11 +1006,17 @@
             lax.dynamic_slice_in_dim(grad, lax.rem(place_z + k, outer) * rows, rows, 0)
             for k in range(outer)
         ]
-        return exchanged_sum(blocks, "dp").astype(BF)
+        return blocks[:1] + [rotation(blocks[k], "dp", k) for k in range(1, outer)]
+
+    def row_sum(got):
+        return sum(a.astype(F32) for a in got).astype(BF)
 
     iwg_values = by_rows(mm_tn(u, gpv).astype(BF))
+    gate_rows = to_rows(iwg_gate)
+    if outer > 1:
+        gps, gate_rows, iwg_values[1] = lax.optimization_barrier((gps, gate_rows, iwg_values[1]))
     iwg_shared = by_rows(mm_tn(u, gps).astype(BF))
-    gate_rows, value_rows, shared_rows = (to_rows(a) for a in (iwg_gate, iwg_values, iwg_shared))
+    value_rows, shared_rows = to_rows(row_sum(iwg_values)), to_rows(row_sum(iwg_shared))
     in_weight_grad, norm_rows = run_rows(
         outer_h, gate_rows, value_rows, shared_rows, in_weight, norm_gain.astype(F32)[:, None]
     )
@@ -988,22 +1030,14 @@
     rs_own = lax.rsqrt(jnp.mean(rows_float * rows_float, axis=1, keepdims=True) + EPSILON)
     block_out = (rows_float + (alive * r_own)[:, None] * branch.astype(F32)).astype(BF)
     unit = rows_float * rs_own
-    scaled = f * norm_full[None, :]
+    scaled = f.astype(F32) * norm_full[None, :]
     hidden_grad = out_cotangent.astype(F32) + rs_own * (
         scaled - unit * jnp.mean(scaled * unit, axis=1, keepdims=True)
     )
 
-    skip_part = jnp.sum(skip_sums.reshape(local_heads, P_SIZE), axis=1)
-    parts = (
-        conv_sums[: TAPS + 1, :lanes_v].reshape(-1),
-        conv_sums[: TAPS + 1, lanes_v:].reshape(-1),
-        head_sums[0:2, :local_heads].reshape(-1),
-        skip_part,
-        ggg.reshape(-1),
-    )
-    counts = [a.shape[0] for a in parts]
-    bundle = lax.psum(jnp.concatenate(parts), "dp")
-    bundle = lax.all_gather(bundle, "fsdp", axis=0, tiled=False)
+    bundle = exchanged_sum([bundle] * outer, "dp")
+    bundle = jnp.broadcast_to(bundle[None], (inner, *bundle.shape))
+    bundle = lax.all_to_all(bundle, "fsdp", 0, 0, tiled=True).reshape(inner, -1)
     stops = [sum(counts[: i + 1]) for i in range(len(counts))]
     cuts = [bundle[:, stop - size : stop] for stop, size in zip(stops, counts)]
     conv_values = from_places(cuts[0].reshape(inner, TAPS + 1, lanes_v), 1, P_SIZE)

time: 701 us -> 678 us (0.967)
  blocking collectives: 110 us -> 31.6 us
  waiting for transfers between devices: 60.6 us -> 97.5 us
  starting transfers between devices: 97.9 us -> 121 us
  local copies, waits for them, and re-layouts: 82.5 us -> 67.6 us
    ppermute x15 -> x24, waiting for transfers between devices: 9.49 us -> 62 us  [rotation(): lax.ppermute(block, axis, [(i, (i + k) % count) for i in range(count)])]
    all_gather x3 -> x0, blocking collectives: 37.3 us -> none  [the longest x1 14.9 us: body(): bundle = lax.all_gather(bundle, 'fsdp', axis=0, tiled=False)]
    ppermute x15 -> x24, starting transfers between devices: 37.9 us -> 73 us  [rotation(): lax.ppermute(block, axis, [(i, (i + k) % count) for i in range(count)])]
    psum x1 -> x0, blocking collectives: 31.1 us -> none  [body(): bundle = lax.psum(jnp.concatenate(parts), 'dp')]
    ppermute x6 -> x3, starting transfers between devices: 30.1 us -> 12.8 us  [relay_blocks(): left = lax.ppermute(left, axis, [(i + 1, i) for i in range(count - 1)])]
    all_to_all x1 -> x3, starting transfers between devices: 5.44 us -> 18.8 us  [the longest x1 6.92 us: body(): bundle = lax.all_to_all(bundle, 'fsdp', 0, 0, tiled=True).reshape(inner, -1)]
    ppermute x6 -> x3, waiting for transfers between devices: 34.9 us -> 21.7 us  [relay_blocks(): right = lax.ppermute(right, axis, [(i, i + 1) for i in range(count - 1)])]
    all_to_all x3, waiting for transfers between devices: 13.2 us -> 0.01 us  [to_rows(): return lax.all_to_all(mine, 'fsdp', 0, 0, tiled=True)]
  transfers between devices with their start and end apart: 35 -> 40, of which waited for: 8 -> 10; matrix products, arithmetic and copies ran while one was open for 17% -> 17% of each run, Pallas kernels for 40% -> 42%
where the time goes in v2:
time: 678 us; the launch traced here: 667 us
  Pallas kernels  278 us (41%)
  starting transfers between devices  121 us (18%)
  waiting for transfers between devices  97.5 us (14%)
  local copies, waits for them, and re-layouts  67.6 us (10%)
  blocking collectives  31.6 us (5%)
  matrix products  31 us (5%)
  other arithmetic  24.5 us (4%)
  between operations  15.2 us (2%)
    pallas_call x1, Pallas kernels, run_backward(): pl.pallas_call(backward_kernel, grid_spec=pltpu.PrefetchScalarGridSpec(nu...  104 us
    ppermute x24, starting transfers between devices, rotation(): lax.ppermute(block, axis, [(i, (i + k) % count) for i in range(count)])  73 us
    pallas_call x1, Pallas kernels, run_forward(): pl.pallas_call(forward_kernel, grid_spec=pltpu.PrefetchScalarGridSpec(num...  67.7 us
    ppermute x24, waiting for transfers between devices, rotation(): lax.ppermute(block, axis, [(i, (i + k) % count) for i in range(count)])  62 us
    pallas_call x1, Pallas kernels, run_gate_back(): pl.pallas_call(functools.partial(gate_back_kernel, outer), grid_spec=pltp...  45.1 us
    pallas_call x1, Pallas kernels, run_gate(): pl.pallas_call(gate_kernel, grid=(total // STRETCH,), in_specs=[tokens(de...  29.9 us
    dot_general x2, matrix products, mm_tn(): lax.dot_general(a, b, (((0,), (0,)), ((), ())), preferred_element_type=F32)  29.7 us
    pallas_call x1, Pallas kernels, run_pull(): pl.pallas_call(pull_kernel, grid_spec=pltpu.PrefetchScalarGridSpec(num_sc...  27.5 us
  transfers between devices with their start and end apart: 40, of which 10 were waited for; matrix products, arithmetic and copies ran while one was open for 17% of the time, Pallas kernels for 42%

profile of v2, /device:TPU:30, one launch (start us, length us, event | category | flops | bytes accessed | tf_op | source)
XLA Modules:
  0.0 667.1 jit_solution(5613229452796439517)
XLA Ops:
  10.0 11.4 %all_to_all.35 = bf16[8,64,512]{2,1,0:T(8,128)(2,1)S(1)} all-to-all(bf16[8,64,512]{2,1,0:T(8,128)(2,1)S(1)} %reshape.211), channel_id=1, replica_groups=mesh['dp'=4,'fsdp'=8] {'fsdp'}, dimensions={0} | all-to-all | bytes 1048576 | tf_op jit(solution)/shard_map/all_to_all | solution.py:898
  31.8 6.5 all-to-all-start
  44.0 7.3 %collective-permute-done.4 = bf16[512,512]{1,0:T(8,128)(2,1)} collective-permute-done((bf16[512,512]{1,0:T(8,128)(2,1)S(1)}, bf16[512,512]{1,0:T(8,128)(2,1)}, u32[]{:S(2)}, u32[]{:S(2)}) %collective-permute-start.4) | collective-permute-done | bytes 524320 | tf_op jit(solution)/shard_map/ppermute | solution.py:750
  51.4 5.3 collective-permute-start.6
  60.1 5.7 all-to-all-done
  65.8 5.4 all-to-all-start.2
  81.1 3.7 reshape.214
  88.6 5.4 collective-permute-start.8
  104.7 21.7 %collective-permute-done.7 = bf16[512,512]{1,0:T(8,128)(2,1)} collective-permute-done((bf16[512,512]{1,0:T(8,128)(2,1)}, bf16[512,512]{1,0:T(8,128)(2,1)}, u32[]{:S(2)}, u32[]{:S(2)}) %collective-permute-start.7) | collective-permute-done | bytes 524320 | tf_op jit(solution)/shard_map/ppermute | solution.py:749
  127.5 13.5 %collective-permute-start.13 = (bf16[128,2048]{1,0:T(8,128)(2,1)}, bf16[128,2048]{1,0:T(8,128)(2,1)}, u32[]{:S(2)}, u32[]{:S(2)}) collective-permute-start(bf16[128,2048]{1,0:T(8,128)(2,1)} %param.28), channel_id=1, source_target_pairs={{0,16},{8,24},{16,0},{24,8},{1,17},{9,25},{17,1},{25,9},{2,18},{10... | collective-permute-start | bytes 1572872 | tf_op jit(solution)/shard_map/ppermute | solution.py:758
  143.5 67.7 %shard_map.257 = (bf16[4096,2048]{1,0:T(8,128)(2,1)}, f32[4096,768]{1,0:T(8,128)}, f32[4096,128]{1,0:T(8,128)}, f32[4096,512]{1,0:T(8,128)}, f32[16,128,512]{2,1,0:T(8,128)}) custom-call(s32[16]{0:T(128)} %convert_element_type.134.starts, bf16[4096,2048]{1,0:T(8,128)(2,1)} %all-gather.3.cloned.1.call-done.hid, f32[1,2048]{1,0:T(1,128)} %broadcast_in_dim_reshape.10.gain, ...), custom_call_target="tpu_custom_call" | custom-call | flops 51539607552 | tf_op jit(solution)/shard_map/pallas_call | solution.py:536
  221.4 29.9 %shard_map.258 = (bf16[4096,2048]{1,0:T(8,128)(2,1)}, f32[4096,512]{1,0:T(8,128)}, f32[8,4096]{1,0:T(8,128)}) custom-call(bf16[4096,2048]{1,0:T(8,128)(2,1)} %get-tuple-element.59.u.hid, bf16[2560,512]{1,0:T(8,128)(2,1)} %copy-done.1, bf16[640,2048]{1,0:T(8,128)(2,1)} %copy-done.2, f32[4096,512]{1,0:T(8,128)} %get-tuple-element.61.mixed, ...), custom_call_target="tpu_custom_call" | custom-call | flops 8589934592 | tf_op jit(solution)/shard_map/pallas_call | solution.py:583
  253.0 27.5 %shard_map.259 = (f32[4096,512]{1,0:T(8,128)}, f32[8,4096]{1,0:T(8,128)}) custom-call(s32[16]{0:T(128)} %copy-done.18, bf16[4096,2048]{1,0:T(8,128)(2,1)} %all-gather.5.cloned.1.call-done.cot, bf16[640,2048]{1,0:T(8,128)(2,1)} %copy-done.2, f32[4096,512]{1,0:T(8,128)} %get-tuple-element.73.gate, f32[4096,512]{1,0:T(8,128)} %get-tuple-element.61.mixed, ...), custom_call_target="tpu_custom_call" | custom-call | flops 85899344 | tf_op jit(solution)/shard_map/pallas_call | solution.py:611
  281.5 20.3 %psum.7 = f32[2,4096]{1,0:T(2,128)S(1)} all-reduce(f32[2,4096]{1,0:T(2,128)S(1)} %pad_maximum_fusion.1), channel_id=1, replica_groups=mesh['dp'=4,'fsdp'=8] {'fsdp'}, use_global_device_ids=true, to_apply=%region_0.1 | all-reduce | flops 8192 | bytes 65536 | tf_op jit(solution)/shard_map/psum | solution.py:960
  303.9 45.1 %shard_map.260 = (f32[4096,512]{1,0:T(8,128)}, bf16[4096,512]{1,0:T(8,128)(2,1)}, f32[1,512]{1,0:T(1,128)}, bf16[512,512]{1,0:T(8,128)(2,1)}, bf16[512,512]{1,0:...) custom-call(s32[17]{0:T(128)} %pad_add_fusion.lengths, ...), custom_call_target="tpu_custom_call" | custom-call | flops 85899344 | tf_op jit(solution)/shard_map/pallas_call | solution.py:640
  351.6 3.8 collective-permute-start.15
  355.4 9.1 %collective-permute-done.18 = bf16[512,512]{1,0:T(8,128)(2,1)S(1)} collective-permute-done((bf16[512,512]{1,0:T(8,128)(2,1)}, bf16[512,512]{1,0:T(8,128)(2,1)S(1)}, u32[]{:S(2)}, u32[]{:S(2)}) %collective-permute-start.18) | collective-permute-done | bytes 524320 | tf_op jit(solution)/shard_map/ppermute | solution.py:758
  364.5 23.4 %collective-permute-start.17 = (bf16[128,2048]{1,0:T(8,128)(2,1)}, bf16[128,2048]{1,0:T(8,128)(2,1)}, u32[]{:S(2)}, u32[]{:S(2)}) collective-permute-start(bf16[128,2048]{1,0:T(8,128)(2,1)} %get-tuple-element.86), channel_id=1, source_target_pairs={{0,24},{8,0},{16,8},{24,16},{1,25},{9,1},{17,9},{25,17},{2,26},{10... | collective-permute-start | bytes 1572872 | tf_op jit(solution)/shard_map/ppermute | solution.py:758
  387.9 104.4 %shard_map.261 = (bf16[4096,2048]{1,0:T(8,128)(2,1)}, bf16[4096,512]{1,0:T(8,128)(2,1)}, bf16[4096,384]{1,0:T(8,128)(2,1)}, f32[8,768]{1,0:T(8,128)}, f32[8,128]{1,0:T(8,128)}, /*index=5*/f32[1,512]{1,0:T(1,128)}) custom-call(s32[16]{0:T(128)} %convert_element_type.134.starts, f32[4096,768]{1,0:T(8,128)} %get-tuple-element.75.xin.xprev, ...), custom_call_target="tpu_custom_call" | custom-call | flops 85899344 | tf_op jit(solution)/shard_map/pallas_call | solution.py:685
  503.1 3.8 collective-permute-start.27
  506.9 15.9 %convolution_convert_fusion = bf16[2048,512]{1,0:T(8,128)(2,1)} fusion(bf16[4096,2048]{1,0:T(8,128)(2,1)} %get-tuple-element.59.u.hid, bf16[4096,512]{1,0:T(8,128)(2,1)} %get-tuple-element.99), kind=kOutput, calls=%fused_computation.12 | convolution fusion | flops 8590983168 | bytes 23068672 | tf_op jit(solution)/shard_map/dot_general | solution.py:41
  523.5 6.9 %all-to-all-start.6 = ((f32[8,40,128]{2,1,0:T(8,128)}), f32[8,40,128]{2,1,0:T(8,128)S(1)}, u32[]{:S(2)}, u32[]{:S(2)}) async-start(f32[8,40,128]{2,1,0:T(8,128)} %broadcast_in_dim.46), calls=%async_computation.8 | async-start | bytes 327680 | tf_op jit(solution)/shard_map/all_to_all | solution.py:1040
  535.5 3.8 collective-permute-start.21
  539.3 4.4 all-to-all-start.3
  551.0 20.8 %collective-permute-done.21 = bf16[512,512]{1,0:T(8,128)(2,1)} collective-permute-done((bf16[512,512]{1,0:T(8,128)(2,1)}, bf16[512,512]{1,0:T(8,128)(2,1)}, u32[]{:S(2)}, u32[]{:S(2)}) %collective-permute-start.21) | collective-permute-done | bytes 524320 | tf_op jit(solution)/shard_map/ppermute | solution.py:758
  571.9 13.8 %convolution_convert_fusion.1 = bf16[2048,384]{1,0:T(8,128)(2,1)S(1)} fusion(bf16[4096,2048]{1,0:T(8,128)(2,1)} %get-tuple-element.59.u.hid, bf16[4096,384]{1,0:T(8,128)(2,1)} %get-tuple-element.102), kind=kOutput, calls=%fused_computation.13 | convolution fusion | flops 6443237376 | bytes 21495808 | tf_op jit(solution)/shard_map/dot_general | solution.py:41
  589.8 8.2 %collective-permute-start.26 = (bf16[512,384]{1,0:T(8,128)(2,1)S(1)}, bf16[512,384]{1,0:T(8,128)(2,1)}, u32[]{:S(2)}, u32[]{:S(2)}) collective-permute-start(bf16[512,384]{1,0:T(8,128)(2,1)S(1)} %get-tuple-element.117), channel_id=1, source_target_pairs={{0,24},{8,0},{16,8},{24,16},{1,25},{9,1},{17,9},{25,17},{2,26},{10... | collective-permute-start | bytes 1179656 | tf_op jit(solution)/shard_map/ppermute | solution.py:758
  602.2 4.2 all-to-all-start.4
  608.6 8.9 %collective-permute-done.26 = bf16[512,384]{1,0:T(8,128)(2,1)} collective-permute-done((bf16[512,384]{1,0:T(8,128)(2,1)S(1)}, bf16[512,384]{1,0:T(8,128)(2,1)}, u32[]{:S(2)}, u32[]{:S(2)}) %collective-permute-start.26) | collective-permute-done | bytes 393248 | tf_op jit(solution)/shard_map/ppermute | solution.py:758
  617.5 16.6 %collective-permute-done.25 = bf16[512,384]{1,0:T(8,128)(2,1)} collective-permute-done((bf16[512,384]{1,0:T(8,128)(2,1)S(1)}, bf16[512,384]{1,0:T(8,128)(2,1)}, u32[]{:S(2)}, u32[]{:S(2)}) %collective-permute-start.25) | collective-permute-done | bytes 393248 | tf_op jit(solution)/shard_map/ppermute | solution.py:758
  636.5 4.2 all-to-all-start.5
  655.3 4.9 fusion.5
  (273 shorter events, 118.3 us)
Async XLA Ops:
  7.2 136.1 %all-gather.3.cloned.1.call-start = ((), (), s32[]{:S(2)}) async-start(), calls=%async_computation.9 | async-start | bytes 18874368 | tf_op jit(solution)/shard_map/all_gather | solution.py:870
  7.9 245.1 %all-gather.5.cloned.1.call-start = ((), (), s32[]{:S(2)}) async-start(), calls=%async_computation.10 | async-start | bytes 18874368 | tf_op jit(solution)/shard_map/all_gather | solution.py:903
  31.8 34.0 %all-to-all-start = ((bf16[8,320,320]{2,1,0:T(8,128)(2,1)}), bf16[8,320,320]{2,1,0:T(8,128)(2,1)}, u32[]{:S(2)}, u32[]{:S(2)}) async-start(bf16[8,320,320]{2,1,0:T(8,128)(2,1)} %broadcast_in_dim.40), calls=%async_computation | async-start | bytes 3932160 | tf_op jit(solution)/shard_map/all_to_all | solution.py:895
  51.4 37.2 %collective-permute-start.6 = (bf16[512,512]{1,0:T(8,128)(2,1)}, bf16[512,512]{1,0:T(8,128)(2,1)}, u32[]{:S(2)}, u32[]{:S(2)}) collective-permute-start(bf16[512,512]{1,0:T(8,128)(2,1)} %collective-permute-done.4), channel_id=1, source_target_pairs={{8,0},{16,8},{24,16},{9,1},{17,9},{25,17},{10,2},{18,10},{26,18},{... | collective-permute-start | bytes 1572872 | tf_op jit(solution)/shard_map/ppermute | solution.py:750
  56.7 30.5 %collective-permute-start.5 = (bf16[512,512]{1,0:T(8,128)(2,1)}, bf16[512,512]{1,0:T(8,128)(2,1)}, u32[]{:S(2)}, u32[]{:S(2)}) collective-permute-start(bf16[512,512]{1,0:T(8,128)(2,1)} %collective-permute-done.3), channel_id=1, source_target_pairs={{0,8},{8,16},{16,24},{1,9},{9,17},{17,25},{2,10},{10,18},{18,26},{... | collective-permute-start | bytes 1572872 | tf_op jit(solution)/shard_map/ppermute | solution.py:749
  65.8 28.8 %all-to-all-start.2 = ((bf16[8,64,512]{2,1,0:T(8,128)(2,1)}), bf16[8,64,512]{2,1,0:T(8,128)(2,1)S(1)}, u32[]{:S(2)}, u32[]{:S(2)}) async-start(bf16[8,64,512]{2,1,0:T(8,128)(2,1)} %reshape.221), calls=%async_computation.2 | async-start | bytes 1048576 | tf_op jit(solution)/shard_map/all_to_all | solution.py:900
  71.2 429.2 %reduce-scatter.3.cloned.1.call-start = ((), (), s32[]{:S(2)}) async-start(), calls=%async_computation.11 | async-start | bytes 18874368 | tf_op jit(solution)/shard_map/reduce_scatter | solution.py:964
  87.2 39.2 %collective-permute-start.7 = (bf16[512,512]{1,0:T(8,128)(2,1)}, bf16[512,512]{1,0:T(8,128)(2,1)}, u32[]{:S(2)}, u32[]{:S(2)}) collective-permute-start(bf16[512,512]{1,0:T(8,128)(2,1)} %collective-permute-done.5), channel_id=1, source_target_pairs={{0,8},{8,16},{16,24},{1,9},{9,17},{17,25},{2,10},{10,18},{18,26},{... | collective-permute-start | bytes 1572872 | tf_op jit(solution)/shard_map/ppermute | solution.py:749
  88.6 38.9 %collective-permute-start.8 = (bf16[512,512]{1,0:T(8,128)(2,1)}, bf16[512,512]{1,0:T(8,128)(2,1)}, u32[]{:S(2)}, u32[]{:S(2)}) collective-permute-start(bf16[512,512]{1,0:T(8,128)(2,1)} %collective-permute-done.6), channel_id=1, source_target_pairs={{8,0},{16,8},{24,16},{9,1},{17,9},{25,17},{10,2},{18,10},{26,18},{... | collective-permute-start | bytes 1572872 | tf_op jit(solution)/shard_map/ppermute | solution.py:750
  94.6 47.5 %collective-permute-start.14 = (bf16[128,2048]{1,0:T(8,128)(2,1)}, bf16[128,2048]{1,0:T(8,128)(2,1)}, u32[]{:S(2)}, u32[]{:S(2)}) collective-permute-start(bf16[128,2048]{1,0:T(8,128)(2,1)} %param.28), channel_id=1, source_target_pairs={{0,24},{8,0},{16,8},{24,16},{1,25},{9,1},{17,9},{25,17},{2,26},{10... | collective-permute-start | bytes 1572872 | tf_op jit(solution)/shard_map/ppermute | solution.py:758
  98.2 113.1 %collective-permute-start.11 = (bf16[512,512]{1,0:T(8,128)(2,1)S(1)}, bf16[512,512]{1,0:T(8,128)(2,1)}, u32[]{:S(2)}, u32[]{:S(2)}) collective-permute-start(bf16[512,512]{1,0:T(8,128)(2,1)S(1)} %bitcast.116), channel_id=1, source_target_pairs={{0,24},{8,0},{16,8},{24,16},{1,25},{9,1},{17,9},{25,17},{2,26},{10... | collective-permute-start | bytes 1572872 | tf_op jit(solution)/shard_map/ppermute | solution.py:758
  99.2 112.1 %collective-permute-start.10 = (bf16[512,512]{1,0:T(8,128)(2,1)S(1)}, bf16[512,512]{1,0:T(8,128)(2,1)}, u32[]{:S(2)}, u32[]{:S(2)}) collective-permute-start(bf16[512,512]{1,0:T(8,128)(2,1)S(1)} %bitcast.117), channel_id=1, source_target_pairs={{0,16},{8,24},{16,0},{24,8},{1,17},{9,25},{17,1},{25,9},{2,18},{10... | collective-permute-start | bytes 1572872 | tf_op jit(solution)/shard_map/ppermute | solution.py:758
  126.4 84.9 %collective-permute-start.9 = (bf16[512,512]{1,0:T(8,128)(2,1)S(1)}, bf16[512,512]{1,0:T(8,128)(2,1)}, u32[]{:S(2)}, u32[]{:S(2)}) collective-permute-start(bf16[512,512]{1,0:T(8,128)(2,1)S(1)} %bitcast.118), channel_id=1, source_target_pairs={{0,8},{8,16},{16,24},{24,0},{1,9},{9,17},{17,25},{25,1},{2,10},{10... | collective-permute-start | bytes 1572872 | tf_op jit(solution)/shard_map/ppermute | solution.py:758
  127.5 83.8 %collective-permute-start.13 = (bf16[128,2048]{1,0:T(8,128)(2,1)}, bf16[128,2048]{1,0:T(8,128)(2,1)}, u32[]{:S(2)}, u32[]{:S(2)}) collective-permute-start(bf16[128,2048]{1,0:T(8,128)(2,1)} %param.28), channel_id=1, source_target_pairs={{0,16},{8,24},{16,0},{24,8},{1,17},{9,25},{17,1},{25,9},{2,18},{10... | collective-permute-start | bytes 1572872 | tf_op jit(solution)/shard_map/ppermute | solution.py:758
  142.1 69.2 %collective-permute-start.12 = (bf16[128,2048]{1,0:T(8,128)(2,1)}, bf16[128,2048]{1,0:T(8,128)(2,1)}, u32[]{:S(2)}, u32[]{:S(2)}) collective-permute-start(bf16[128,2048]{1,0:T(8,128)(2,1)} %param.28), channel_id=1, source_target_pairs={{0,8},{8,16},{16,24},{24,0},{1,9},{9,17},{17,25},{25,1},{2,10},{10... | collective-permute-start | bytes 1572872 | tf_op jit(solution)/shard_map/ppermute | solution.py:758
  251.3 401.1 %reduce-scatter.5.cloned.1.call-start = ((), (), s32[]{:S(2)}) async-start(), calls=%async_computation.12 | async-start | bytes 18874368 | tf_op jit(solution)/shard_map/reduce_scatter | solution.py:1001
  350.2 146.6 %collective-permute-start.19 = (bf16[512,512]{1,0:T(8,128)(2,1)}, bf16[512,512]{1,0:T(8,128)(2,1)S(1)}, u32[]{:S(2)}, u32[]{:S(2)}) collective-permute-start(bf16[512,512]{1,0:T(8,128)(2,1)} %get-tuple-element.89), channel_id=1, source_target_pairs={{0,16},{8,24},{16,0},{24,8},{1,17},{9,25},{17,1},{25,9},{2,18},{10... | collective-permute-start | bytes 1572872 | tf_op jit(solution)/shard_map/ppermute | solution.py:758
  351.6 145.2 %collective-permute-start.20 = (bf16[512,512]{1,0:T(8,128)(2,1)}, bf16[512,512]{1,0:T(8,128)(2,1)S(1)}, u32[]{:S(2)}, u32[]{:S(2)}) collective-permute-start(bf16[512,512]{1,0:T(8,128)(2,1)} %get-tuple-element.90), channel_id=1, source_target_pairs={{0,24},{8,0},{16,8},{24,16},{1,25},{9,1},{17,9},{25,17},{2,26},{10... | collective-permute-start | bytes 1572872 | tf_op jit(solution)/shard_map/ppermute | solution.py:758
  351.6 146.3 %collective-permute-start.15 = (bf16[128,2048]{1,0:T(8,128)(2,1)}, bf16[128,2048]{1,0:T(8,128)(2,1)S(1)}, u32[]{:S(2)}, u32[]{:S(2)}) collective-permute-start(bf16[128,2048]{1,0:T(8,128)(2,1)} %get-tuple-element.84), channel_id=1, source_target_pairs={{0,8},{8,16},{16,24},{24,0},{1,9},{9,17},{17,25},{25,1},{2,10},{10... | collective-permute-start | bytes 1572872 | tf_op jit(solution)/shard_map/ppermute | solution.py:758
  355.4 142.4 %collective-permute-start.16 = (bf16[128,2048]{1,0:T(8,128)(2,1)}, bf16[128,2048]{1,0:T(8,128)(2,1)}, u32[]{:S(2)}, u32[]{:S(2)}) collective-permute-start(bf16[128,2048]{1,0:T(8,128)(2,1)} %get-tuple-element.85), channel_id=1, source_target_pairs={{0,16},{8,24},{16,0},{24,8},{1,17},{9,25},{17,1},{25,9},{2,18},{10... | collective-permute-start | bytes 1572872 | tf_op jit(solution)/shard_map/ppermute | solution.py:758
  364.5 133.3 %collective-permute-start.17 = (bf16[128,2048]{1,0:T(8,128)(2,1)}, bf16[128,2048]{1,0:T(8,128)(2,1)}, u32[]{:S(2)}, u32[]{:S(2)}) collective-permute-start(bf16[128,2048]{1,0:T(8,128)(2,1)} %get-tuple-element.86), channel_id=1, source_target_pairs={{0,24},{8,0},{16,8},{24,16},{1,25},{9,1},{17,9},{25,17},{2,26},{10... | collective-permute-start | bytes 1572872 | tf_op jit(solution)/shard_map/ppermute | solution.py:758
  503.1 19.7 %collective-permute-start.29 = (f32[40,128]{1,0:T(8,128)S(1)}, f32[40,128]{1,0:T(8,128)S(1)}, u32[]{:S(2)}, u32[]{:S(2)}) collective-permute-start(f32[40,128]{1,0:T(8,128)S(1)} %pad_bitcast_fusion), channel_id=1, source_target_pairs={{0,24},{8,0},{16,8},{24,16},{1,25},{9,1},{17,9},{25,17},{2,26},{10... | collective-permute-start | bytes 61448 | tf_op jit(solution)/shard_map/ppermute | solution.py:758
  503.1 19.7 %collective-permute-start.28 = (f32[40,128]{1,0:T(8,128)S(1)}, f32[40,128]{1,0:T(8,128)S(1)}, u32[]{:S(2)}, u32[]{:S(2)}) collective-permute-start(f32[40,128]{1,0:T(8,128)S(1)} %pad_bitcast_fusion), channel_id=1, source_target_pairs={{0,16},{8,24},{16,0},{24,8},{1,17},{9,25},{17,1},{25,9},{2,18},{10... | collective-permute-start | bytes 61448 | tf_op jit(solution)/shard_map/ppermute | solution.py:758
  503.1 19.7 %collective-permute-start.27 = (f32[40,128]{1,0:T(8,128)S(1)}, f32[40,128]{1,0:T(8,128)S(1)}, u32[]{:S(2)}, u32[]{:S(2)}) collective-permute-start(f32[40,128]{1,0:T(8,128)S(1)} %pad_bitcast_fusion), channel_id=1, source_target_pairs={{0,8},{8,16},{16,24},{24,0},{1,9},{9,17},{17,25},{25,1},{2,10},{10... | collective-permute-start | bytes 61448 | tf_op jit(solution)/shard_map/ppermute | solution.py:758
  533.1 66.5 %collective-permute-start.22 = (bf16[512,512]{1,0:T(8,128)(2,1)}, bf16[512,512]{1,0:T(8,128)(2,1)}, u32[]{:S(2)}, u32[]{:S(2)}) collective-permute-start(bf16[512,512]{1,0:T(8,128)(2,1)} %get-tuple-element.111), channel_id=1, source_target_pairs={{0,16},{8,24},{16,0},{24,8},{1,17},{9,25},{17,1},{25,9},{2,18},{10... | collective-permute-start | bytes 1572872 | tf_op jit(solution)/shard_map/ppermute | solution.py:758
  535.5 64.1 %collective-permute-start.23 = (bf16[512,512]{1,0:T(8,128)(2,1)}, bf16[512,512]{1,0:T(8,128)(2,1)}, u32[]{:S(2)}, u32[]{:S(2)}) collective-permute-start(bf16[512,512]{1,0:T(8,128)(2,1)} %get-tuple-element.112), channel_id=1, source_target_pairs={{0,24},{8,0},{16,8},{24,16},{1,25},{9,1},{17,9},{25,17},{2,26},{10... | collective-permute-start | bytes 1572872 | tf_op jit(solution)/shard_map/ppermute | solution.py:758
  535.5 36.4 %collective-permute-start.21 = (bf16[512,512]{1,0:T(8,128)(2,1)}, bf16[512,512]{1,0:T(8,128)(2,1)}, u32[]{:S(2)}, u32[]{:S(2)}) collective-permute-start(bf16[512,512]{1,0:T(8,128)(2,1)} %get-tuple-element.113), channel_id=1, source_target_pairs={{0,8},{8,16},{16,24},{24,0},{1,9},{9,17},{17,25},{25,1},{2,10},{10... | collective-permute-start | bytes 1572872 | tf_op jit(solution)/shard_map/ppermute | solution.py:758
  539.3 32.6 %all-to-all-start.3 = ((bf16[8,64,512]{2,1,0:T(8,128)(2,1)}), bf16[8,64,512]{2,1,0:T(8,128)(2,1)}, u32[]{:S(2)}, u32[]{:S(2)}) async-start(bf16[8,64,512]{2,1,0:T(8,128)(2,1)} %bitcast.25), calls=%async_computation.5 | async-start | bytes 1048576 | tf_op jit(solution)/shard_map/all_to_all | solution.py:981
  587.7 20.9 %collective-permute-start.24 = (bf16[512,384]{1,0:T(8,128)(2,1)}, bf16[512,384]{1,0:T(8,128)(2,1)}, u32[]{:S(2)}, u32[]{:S(2)}) collective-permute-start(bf16[512,384]{1,0:T(8,128)(2,1)} %get-tuple-element.116), channel_id=1, source_target_pairs={{0,8},{8,16},{16,24},{24,0},{1,9},{9,17},{17,25},{25,1},{2,10},{10... | collective-permute-start | bytes 1179656 | tf_op jit(solution)/shard_map/ppermute | solution.py:758
  589.8 27.6 %collective-permute-start.26 = (bf16[512,384]{1,0:T(8,128)(2,1)S(1)}, bf16[512,384]{1,0:T(8,128)(2,1)}, u32[]{:S(2)}, u32[]{:S(2)}) collective-permute-start(bf16[512,384]{1,0:T(8,128)(2,1)S(1)} %get-tuple-element.117), channel_id=1, source_target_pairs={{0,24},{8,0},{16,8},{24,16},{1,25},{9,1},{17,9},{25,17},{2,26},{10... | collective-permute-start | bytes 1179656 | tf_op jit(solution)/shard_map/ppermute | solution.py:758
  598.1 36.1 %collective-permute-start.25 = (bf16[512,384]{1,0:T(8,128)(2,1)S(1)}, bf16[512,384]{1,0:T(8,128)(2,1)}, u32[]{:S(2)}, u32[]{:S(2)}) collective-permute-start(bf16[512,384]{1,0:T(8,128)(2,1)S(1)} %get-tuple-element.118), channel_id=1, source_target_pairs={{0,16},{8,24},{16,0},{24,8},{1,17},{9,25},{17,1},{25,9},{2,18},{10... | collective-permute-start | bytes 1179656 | tf_op jit(solution)/shard_map/ppermute | solution.py:758
  602.2 34.3 %all-to-all-start.4 = ((bf16[8,64,512]{2,1,0:T(8,128)(2,1)}), bf16[8,64,512]{2,1,0:T(8,128)(2,1)S(1)}, u32[]{:S(2)}, u32[]{:S(2)}) async-start(bf16[8,64,512]{2,1,0:T(8,128)(2,1)} %bitcast.26), calls=%async_computation.6 | async-start | bytes 1048576 | tf_op jit(solution)/shard_map/all_to_all | solution.py:981
  (37 other events, 545.2 us)
Sparse Core Ops, SparseCore 0:
  9.9 111.1 all-gather.2
  123.0 89.8 all-gather.4
  251.5 116.2 reduce-scatter.2
  500.5 129.0 reduce-scatter.4
